TPU v7x, 512 devices: a whole 4x8x8 slice. The times are simulated.
512 devices in a mesh: gy: 16 (over z, core), gx: 32 (over y, x).
Axes of the slice: x: 4, y: 8, z: 8, core: 2. Of those that a mesh axis runs over, the one named last changes fastest.
Arguments:
- mask: float32 [640, 4096], P('gy', 'gx'), may hold values from 0 to 1
- target: int32 [640, 4096], P('gy', 'gx'), may hold values 0 or 1
- kernels: bfloat16 [24, 35, 35], replicated, may hold values from -0.15625 to 0.15625
- offsets: int32 [8, 2], replicated, may hold values from -8 to 8, as said below
- load_weights: float32 [8], replicated, may hold values from 0.2 to 1
Outputs:
- update: float32 [640, 4096], P('gy', 'gx')
- loss: float32 [], replicated
Inputs may be any that keep to these rules, and one draw needn't show every extreme that they name: `offsets`: some offset has row component 8 and some has column component -8.
All inputs are finite; a program needn't handle non-finite values. No bound on the sum of `target` on one device may be relied on, other than what follows from the above.
Results may differ from a plain program's by a relative error of at most 0.002.
Values may be sent and summed in bfloat16 or wider, within the bound.
A program may use at most 64 MiB of HBM per device.

v0:
```python
import jax
import jax.numpy as jnp
from jax import lax
from jax.sharding import Mesh
from jax.sharding import PartitionSpec as P

KERNELS = 12
REACH = 8
LOAD_TAPS = 8
GY = ("gy_0", "gy_1")
GX = ("gx_0", "gx_1")
GY_GX = ("gy_0", "gy_1", "gx_0", "gx_1")


SMOOTH_TAPS = (0.0625, 0.25, 0.375, 0.25, 0.0625)
SHARPNESS = 4.0
THRESHOLD = 0.65
LOADING_GAIN = 0.5
ROW_BLOCK = 8


def with_halo(block, sides, width):
    for axis, dim in sides:
        count = lax.axis_size(axis)
        forward = [(i, i + 1) for i in range(count - 1)]
        backward = [(target, source) for source, target in forward]
        low = lax.ppermute(
            lax.slice_in_dim(block, block.shape[dim] - width, None, axis=dim), axis, forward
        )
        high = lax.ppermute(lax.slice_in_dim(block, 0, width, axis=dim), axis, backward)
        block = jnp.concatenate([low, block, high], axis=dim)
    return block


def one_axis_at_a_time(value, axes):
    for axis in axes:
        value = lax.psum(value, axis)
    return value


def smooth_valid(padded, out_rows, out_cols):
    partial_rows = sum((SMOOTH_TAPS[a] * padded[a : a + out_rows, :] for a in range(5)))
    return sum((SMOOTH_TAPS[b] * partial_rows[:, b : b + out_cols] for b in range(5)))


def forward_field(extended, kernels, out_rows, out_cols):
    channels, taps = (kernels.shape[0], kernels.shape[1])
    blocks = -(-out_rows // ROW_BLOCK)
    flat_kernels = kernels.reshape(channels, taps * taps)

    def one_block(block_index, total):
        start = block_index * ROW_BLOCK
        band = lax.dynamic_slice_in_dim(extended, start, ROW_BLOCK + taps - 1, 0)
        across = jnp.stack([band[:, b : b + out_cols] for b in range(taps)])
        patches = jnp.stack([across[:, a : a + ROW_BLOCK, :] for a in range(taps)])
        patches = patches.reshape(taps * taps, ROW_BLOCK, out_cols)
        piece = jnp.einsum("ck,kyx->cyx", flat_kernels, patches, preferred_element_type=jnp.float32)
        return lax.dynamic_update_slice_in_dim(total, piece, start, 1)

    empty = jnp.zeros((channels, blocks * ROW_BLOCK, out_cols), jnp.float32)
    result = lax.fori_loop(0, blocks, one_block, empty)
    return result


def adjoint_field(products, kernels, out_rows, out_cols):
    taps = kernels.shape[1]
    reach = 2 * (taps // 2)

    def one_row(tap_row, total):
        band = lax.dynamic_slice_in_dim(products, reach - tap_row, out_rows, 1)
        row_weights = lax.dynamic_index_in_dim(kernels, tap_row, 1, keepdims=False)
        mixed = jnp.einsum("cb,cyx->byx", row_weights, band, preferred_element_type=jnp.float32)
        return total + sum((mixed[b, :, reach - b : reach - b + out_cols] for b in range(taps)))

    empty = jnp.zeros((out_rows, out_cols), jnp.float32)
    return lax.fori_loop(0, taps, one_row, empty)


def inside_window(first, count, total):
    position = first + jnp.arange(count, dtype=jnp.int32)
    return (position >= 0) & (position < total)


def body(mask, target, kernels, offsets, load_weights):
    tile_rows, tile_cols = mask.shape
    radius = kernels.shape[-1] // 2
    margin = REACH + 2
    total_rows = tile_rows * lax.axis_size(GY)
    total_cols = tile_cols * lax.axis_size(GX)
    first_row = lax.axis_index(GY) * tile_rows
    first_col = lax.axis_index(GX) * tile_cols
    plane = mask.astype(jnp.bfloat16)
    extended = with_halo(plane, ((GY, 0), (GX, 1)), radius)
    field = forward_field(extended, kernels, tile_rows, tile_cols)
    intensity = jnp.sum(field * field, axis=0) / KERNELS
    inten_ext = with_halo(intensity, ((GY, 0), (GX, 1)), margin)
    dense = smooth_valid(inten_ext, tile_rows + 2 * REACH, tile_cols + 2 * REACH)
    inside = (
        inside_window(first_row - REACH, tile_rows + 2 * REACH, total_rows)[:, None]
        & inside_window(first_col - REACH, tile_cols + 2 * REACH, total_cols)[None, :]
    )
    develop = jnp.where(inside, jax.nn.sigmoid(SHARPNESS * (dense - THRESHOLD)), 0.0)
    loading = jnp.zeros((tile_rows, tile_cols), jnp.float32)
    for index in range(LOAD_TAPS):
        shifted = lax.dynamic_slice(
            develop, (REACH + offsets[index, 0], REACH + offsets[index, 1]), (tile_rows, tile_cols)
        )
        loading = loading + load_weights[index] * shifted
    center = develop[REACH : REACH + tile_rows, REACH : REACH + tile_cols]
    printed = center - LOADING_GAIN / LOAD_TAPS * loading
    row_pos = (first_row + jnp.arange(tile_rows, dtype=jnp.int32)).astype(jnp.float32)
    col_pos = (first_col + jnp.arange(tile_cols, dtype=jnp.int32)).astype(jnp.float32)
    weight = (1.0 + 2.0 * row_pos / total_rows)[:, None] * (1.0 + 2.0 * col_pos / total_cols)[
        None, :
    ]
    diff = printed - target.astype(jnp.float32)
    part_loss = jnp.sum(weight * diff * diff)
    resid = 2.0 * weight * diff
    resid_ext = with_halo(resid, ((GY, 0), (GX, 1)), margin)
    back = jnp.zeros((tile_rows + 4, tile_cols + 4), jnp.float32)
    for index in range(LOAD_TAPS):
        shifted = lax.dynamic_slice(
            resid_ext,
            (REACH - offsets[index, 0], REACH - offsets[index, 1]),
            (tile_rows + 4, tile_cols + 4),
        )
        back = back + load_weights[index] * shifted
    slope = (
        resid_ext[REACH : REACH + tile_rows + 4, REACH : REACH + tile_cols + 4]
        - LOADING_GAIN / LOAD_TAPS * back
    )
    nearby = develop[REACH - 2 : REACH + tile_rows + 2, REACH - 2 : REACH + tile_cols + 2]
    inside_near = (
        inside_window(first_row - 2, tile_rows + 4, total_rows)[:, None]
        & inside_window(first_col - 2, tile_cols + 4, total_cols)[None, :]
    )
    dense_grad = jnp.where(inside_near, slope * SHARPNESS * nearby * (1.0 - nearby), 0.0)
    inten_grad = smooth_valid(dense_grad, tile_rows, tile_cols)
    products = (2.0 * field * inten_grad / KERNELS).astype(jnp.bfloat16)
    products = with_halo(products, ((GY, 1), (GX, 2)), radius)
    gradient = adjoint_field(products, kernels, tile_rows, tile_cols)
    totals = (
        one_axis_at_a_time(part_loss, GY_GX),
        one_axis_at_a_time(jnp.sum(gradient * gradient), GY_GX),
    )
    scale = jnp.sqrt(totals[1] / (total_rows * total_cols) + 1e-06)
    update = mask - gradient / scale
    return (update, totals[0])


def solution(mesh):
    finer = Mesh(mesh.devices.reshape(8, 2, 8, 4), ("gy_0", "gy_1", "gx_0", "gx_1"))
    placed = (P(GY, GX), P(GY, GX), P(), P(), P())
    return jax.shard_map(
        body, mesh=finer, in_specs=placed, out_specs=(P(GY, GX), P()), check_vma=False
    )
```

profile of v0, /device:TPU:16, one launch (start us, length us, event | category | flops | bytes accessed | tf_op | source)
XLA Modules:
  0.0 318.7 jit_solution(6249256280259983541)
XLA Ops:
  1.4 1.7 collective-permute-start
  3.1 1.3 collective-permute-start.1
  5.5 2.0 fusion.74
  7.5 1.6 fusion.75
  9.8 3.4 %collective-permute-start.2 = (bf16[74,17]{1,0:T(8,128)(2,1)S(1)}, bf16[74,17]{1,0:T(8,128)(2,1)S(1)}, u32[]{:S(2)}, u32[]{:S(2)}) collective-permute-start(bf16[74,17]{1,0:T(8,128)(2,1)S(1)} %get-tuple-element.281), channel_id=1, source_target_pairs={{0,1},{1,2},{2,3},{3,4},{4,5},{5,6},{6,7},{7,8},{8,9},{9,10},{10,1... | collective-permute-start | bytes 7556 | tf_op jit(solution)/shard_map/ppermute | solution.py:27
  13.2 4.6 %collective-permute-start.3 = (bf16[74,17]{1,0:T(8,128)(2,1)S(1)}, bf16[74,17]{1,0:T(8,128)(2,1)S(1)}, u32[]{:S(2)}, u32[]{:S(2)}) collective-permute-start(bf16[74,17]{1,0:T(8,128)(2,1)S(1)} %get-tuple-element.282), channel_id=1, source_target_pairs={{1,0},{2,1},{3,2},{4,3},{5,4},{6,5},{7,6},{8,7},{9,8},{10,9},{11,1... | collective-permute-start | bytes 7556 | tf_op jit(solution)/shard_map/ppermute | solution.py:30
  19.6 24.7 %while.29 = (s32[]{:T(128)}, f32[24,40,128]{2,0,1:T(8,128)S(1)}, bf16[74,162]{1,0:T(8,128)(2,1)S(1)}, bf16[24,1225]{1,0:T(8,128)(2,1)S(1)}, s32[]{:T(128)}, /*in...) while((s32[]{:T(128)}, f32[24,40,128]{2,0,1:T(8,128)S(1)}, ...), condition=%wide.region_1.0_spmd, body=%wide.region_0.0_spmd.sunk | while | flops 60211240 | bytes 8545892 | solution.py:61
  44.4 4.6 %collective-permute-start.4 = (f32[10,128]{1,0:T(8,128)S(1)}, f32[10,128]{1,0:T(8,128)S(1)}, u32[]{:S(2)}, u32[]{:S(2)}) collective-permute-start(f32[10,128]{1,0:T(8,128)S(1)} %get-tuple-element.279), channel_id=1, source_target_pairs={{0,32},{32,64},{64,96},{96,128},{128,160},{160,192},{192,224},{224... | collective-permute-start | bytes 15368 | tf_op jit(solution)/shard_map/ppermute | solution.py:27
  49.0 1.3 collective-permute-start.5
  70.6 1.9 collective-permute-start.6
  72.6 6.0 %collective-permute-start.7 = (f32[60,10]{1,0:T(8,128)S(1)}, f32[60,10]{1,0:T(8,128)S(1)}, u32[]{:S(2)}, u32[]{:S(2)}) collective-permute-start(f32[60,10]{1,0:T(8,128)S(1)} %get-tuple-element.276), channel_id=1, source_target_pairs={{1,0},{2,1},{3,2},{4,3},{5,4},{6,5},{7,6},{8,7},{9,8},{10,9},{11,1... | collective-permute-start | bytes 7208 | tf_op jit(solution)/shard_map/ppermute | solution.py:30
  78.7 1.4 collective-permute-done.7
  81.1 6.5 %fusion.56 = (f32[]{:T(128)}, f32[40,128]{1,0:T(8,128)S(1)}) fusion(f32[128]{0:T(128)} %multiply_add_fusion, f32[40]{0:T(128)} %multiply_add_fusion.1, s32[40,128]{1,0:T(8,128)S(1)} %copy-done.1, f32[56,144]{1,0:T(8,128)S(1)} %fusion.39, s32[]{:T(128)S(6)} %select_n.152, s32[]{:T(128)S(6)} %select_n.153, f32[]{:T(128)} %bitcast.108, s32[]{:T(128)S(6)} %select_n.150, ...), kind=kLoop, calls=%fused_computation.220 | loop fusion | flops 117759 | bytes 226052 | tf_op jit(solution)/shard_map/reduce_sum | solution.py:117
  88.3 4.0 %collective-permute-start.8 = (f32[10,128]{1,0:T(8,128)S(1)}, f32[10,128]{1,0:T(8,128)S(1)}, u32[]{:S(2)}, u32[]{:S(2)}) collective-permute-start(f32[10,128]{1,0:T(8,128)S(1)} %get-tuple-element.277), channel_id=1, source_target_pairs={{0,32},{32,64},{64,96},{96,128},{128,160},{160,192},{192,224},{224... | collective-permute-start | bytes 15368 | tf_op jit(solution)/shard_map/ppermute | solution.py:27
  92.4 1.3 collective-permute-start.9
  114.0 3.4 %collective-permute-start.10 = (f32[60,10]{1,0:T(8,128)S(1)}, f32[60,10]{1,0:T(8,128)S(1)}, u32[]{:S(2)}, u32[]{:S(2)}) collective-permute-start(f32[60,10]{1,0:T(8,128)S(1)} %get-tuple-element.273), channel_id=1, source_target_pairs={{0,1},{1,2},{2,3},{3,4},{4,5},{5,6},{6,7},{7,8},{8,9},{9,10},{10,1... | collective-permute-start | bytes 7208 | tf_op jit(solution)/shard_map/ppermute | solution.py:27
  117.4 4.5 %collective-permute-start.11 = (f32[60,10]{1,0:T(8,128)S(1)}, f32[60,10]{1,0:T(8,128)S(1)}, u32[]{:S(2)}, u32[]{:S(2)}) collective-permute-start(f32[60,10]{1,0:T(8,128)S(1)} %get-tuple-element.274), channel_id=1, source_target_pairs={{1,0},{2,1},{3,2},{4,3},{5,4},{6,5},{7,6},{8,7},{9,8},{10,9},{11,1... | collective-permute-start | bytes 7208 | tf_op jit(solution)/shard_map/ppermute | solution.py:30
  122.1 1.4 collective-permute-done.11
  123.6 5.2 %fusion.50 = f32[44,132]{1,0:T(8,128)S(1)} fusion(f32[60,148]{1,0:T(8,128)S(1)} %pad_maximum_fusion.3, f32[56,144]{1,0:T(8,128)S(1)} %fusion.39, s32[]{:T(128)S(6)} %select_n.168, s32[]{:T(128)S(6)} %select_n.169, s32[]{:T(128)S(6)} %select_n.166, s32[]{:T(128)S(6)} %select_n.167, s32[]{:T(128)S(6)} %select_n.164, s32[]{:T(128)S(6)} %select_n.165, ...), kind=kLoop, calls=%fused_computation.204 | loop fusion | flops 133584 | bytes 255824 | tf_op jit(solution)/shard_map/jit(_where)/select_n | solution.py:137
  129.1 4.7 %collective-permute-start.12 = (bf16[24,17,128]{2,0,1:T(8,128)(2,1)S(1)}, bf16[24,17,128]{2,0,1:T(8,128)(2,1)S(1)}, u32[]{:S(2)}, u32[]{:S(2)}) collective-permute-start(bf16[24,17,128]{2,0,1:T(8,128)(2,1)S(1)} %get-tuple-element.271), channel_id=1, source_target_pairs={{0,32},{32,64},{64,96},{96,128},{128,160},{160,192},{192,224},{224... | collective-permute-start | bytes 313352 | tf_op jit(solution)/shard_map/ppermute | solution.py:27
  133.8 1.3 collective-permute-start.13
  135.1 4.0 %collective-permute-done.13 = bf16[24,17,128]{2,0,1:T(8,128)(2,1)S(1)} collective-permute-done((bf16[24,17,128]{2,0,1:T(8,128)(2,1)S(1)}, bf16[24,17,128]{2,0,1:T(8,128)(2,1)S(1)}, u32[]{:S(2)}, u32[]{:S(2)}) %collective-permute-start.13) | collective-permute-done | bytes 104480 | tf_op jit(solution)/shard_map/ppermute | solution.py:30
  139.3 3.9 %collective-permute-start.14 = (bf16[24,74,17]{2,0,1:T(8,128)(2,1)S(1)}, bf16[24,74,17]{2,0,1:T(8,128)(2,1)S(1)}, u32[]{:S(2)}, u32[]{:S(2)}) collective-permute-start(bf16[24,74,17]{2,0,1:T(8,128)(2,1)S(1)} %get-tuple-element.269), channel_id=1, source_target_pairs={{0,1},{1,2},{2,3},{3,4},{4,5},{5,6},{6,7},{7,8},{8,9},{9,10},{10,1... | collective-permute-start | bytes 181160 | tf_op jit(solution)/shard_map/ppermute | solution.py:27
  143.2 4.5 %collective-permute-start.15 = (bf16[24,74,17]{2,0,1:T(8,128)(2,1)S(1)}, bf16[24,74,17]{2,0,1:T(8,128)(2,1)S(1)}, u32[]{:S(2)}, u32[]{:S(2)}) collective-permute-start(bf16[24,74,17]{2,0,1:T(8,128)(2,1)S(1)} %get-tuple-element.270), channel_id=1, source_target_pairs={{1,0},{2,1},{3,2},{4,3},{5,4},{6,5},{7,6},{8,7},{9,8},{10,9},{11,1... | collective-permute-start | bytes 181160 | tf_op jit(solution)/shard_map/ppermute | solution.py:30
  147.8 6.7 %collective-permute-done.14 = bf16[24,74,17]{2,0,1:T(8,128)(2,1)S(1)} collective-permute-done((bf16[24,74,17]{2,0,1:T(8,128)(2,1)S(1)}, bf16[24,74,17]{2,0,1:T(8,128)(2,1)S(1)}, u32[]{:S(2)}, u32[]{:S(2)}) %collective-permute-start.14) | collective-permute-done | bytes 60416 | tf_op jit(solution)/shard_map/ppermute | solution.py:27
  154.5 1.7 collective-permute-done.15
  156.8 99.1 %while.30 = (s32[]{:T(128)}, f32[40,128]{1,0:T(8,128)S(1)}, bf16[24,35,35]{2,0,1:T(8,128)(2,1)}, bf16[24,74,162]{2,0,1:T(8,128)(2,1)S(1)}, s32[]{:T(128)}, /*index=5*/s32[]{:T(128)}, s32[]{:T(128)}, s32[]{:T(128)}) while((s32[]{:T(128)}, f32[40,128]{1,0:T(8,128)S(1)}, bf16[24,35,35]{2,0,1:T(8,128)(2,1)}, ...), condition=%wide.region_4.5_spmd.clone, body=%wide.region_3.4_spmd.clone.sunk | while | flops 11070727 | bytes 3596881 | solution.py:76
  156.8 1.1 fusion.90
  159.6 1.1 fusion.90
  162.5 1.1 fusion.90
  165.3 1.1 fusion.90
  171.0 1.1 fusion.90
  173.8 1.1 fusion.90
  176.7 1.1 fusion.90
  179.5 1.1 fusion.90
  182.3 1.1 fusion.90
  185.1 1.1 fusion.90
  188.0 1.1 fusion.90
  190.8 1.1 fusion.90
  193.6 1.1 fusion.90
  196.5 1.1 fusion.90
  199.3 1.1 fusion.90
  202.1 1.1 fusion.90
  204.9 1.1 fusion.90
  207.8 1.1 fusion.90
  210.6 1.1 fusion.90
  213.4 1.1 fusion.90
  216.3 1.1 fusion.90
  219.1 1.1 fusion.90
  221.9 1.1 fusion.90
  224.8 1.1 fusion.90
  227.6 1.1 fusion.90
  230.4 1.1 fusion.90
  233.2 1.1 fusion.90
  238.9 1.1 fusion.90
  241.7 1.1 fusion.90
  244.6 1.1 fusion.90
  247.4 1.1 fusion.90
  250.2 1.1 fusion.90
  253.0 1.1 fusion.90
  256.5 23.8 %all-reduce.1 = (f32[]{:T(128)}, f32[]{:T(128)}) all-reduce(f32[]{:T(128)} %multiply_reduce_fusion.1, f32[]{:T(128)} %get-tuple-element.232), channel_id=1, replica_groups=mesh['gy_0'=8,'gy_1'=2,'gx_0'=8,'gx_1'=4] {'gy_0'}, use_global_device_ids=true, to_apply=%region_6.7 | all-reduce | flops 2 | bytes 16 | tf_op jit(solution)/shard_map/psum | solution.py:37
  280.3 3.1 all-reduce.3
  283.4 20.4 %all-reduce = (f32[]{:T(128)}, f32[]{:T(128)}) all-reduce(f32[]{:T(128)} %get-tuple-element.230, f32[]{:T(128)} %get-tuple-element.231), channel_id=1, replica_groups=mesh['gy_0'=8,'gy_1'=2,'gx_0'=8,'gx_1'=4] {'gx_0'}, use_global_device_ids=true, to_apply=%region_8.9 | all-reduce | flops 2 | bytes 16 | tf_op jit(solution)/shard_map/psum | solution.py:37
  303.8 13.7 %all-reduce.2 = (f32[]{:T(128)}, f32[]{:T(128)}) all-reduce(f32[]{:T(128)} %get-tuple-element.224, f32[]{:T(128)} %get-tuple-element.225), channel_id=1, replica_groups=mesh['gy_0'=8,'gy_1'=2,'gx_0'=8,'gx_1'=4] {'gx_1'}, use_global_device_ids=true, to_apply=%region_9.10 | all-reduce | flops 2 | bytes 16 | tf_op jit(solution)/shard_map/psum | solution.py:37
  (514 shorter events, 94.2 us)
Async XLA Ops:
  1.4 8.3 %collective-permute-start = (bf16[17,128]{1,0:T(8,128)(2,1)S(1)}, bf16[17,128]{1,0:T(8,128)(2,1)S(1)}, u32[]{:S(2)}, u32[]{:S(2)}) collective-permute-start(bf16[17,128]{1,0:T(8,128)(2,1)S(1)} %get-tuple-element.283), channel_id=1, source_target_pairs={{0,32},{32,64},{64,96},{96,128},{128,160},{160,192},{192,224},{224... | collective-permute-start | bytes 13064 | tf_op jit(solution)/shard_map/ppermute | solution.py:27
  3.1 6.5 %collective-permute-start.1 = (bf16[17,128]{1,0:T(8,128)(2,1)S(1)}, bf16[17,128]{1,0:T(8,128)(2,1)S(1)}, u32[]{:S(2)}, u32[]{:S(2)}) collective-permute-start(bf16[17,128]{1,0:T(8,128)(2,1)S(1)} %get-tuple-element.284), channel_id=1, source_target_pairs={{32,0},{64,32},{96,64},{128,96},{160,128},{192,160},{224,192},{256... | collective-permute-start | bytes 13064 | tf_op jit(solution)/shard_map/ppermute | solution.py:30
  9.8 9.7 %collective-permute-start.2 = (bf16[74,17]{1,0:T(8,128)(2,1)S(1)}, bf16[74,17]{1,0:T(8,128)(2,1)S(1)}, u32[]{:S(2)}, u32[]{:S(2)}) collective-permute-start(bf16[74,17]{1,0:T(8,128)(2,1)S(1)} %get-tuple-element.281), channel_id=1, source_target_pairs={{0,1},{1,2},{2,3},{3,4},{4,5},{5,6},{6,7},{7,8},{8,9},{9,10},{10,1... | collective-permute-start | bytes 7556 | tf_op jit(solution)/shard_map/ppermute | solution.py:27
  13.2 6.3 %collective-permute-start.3 = (bf16[74,17]{1,0:T(8,128)(2,1)S(1)}, bf16[74,17]{1,0:T(8,128)(2,1)S(1)}, u32[]{:S(2)}, u32[]{:S(2)}) collective-permute-start(bf16[74,17]{1,0:T(8,128)(2,1)S(1)} %get-tuple-element.282), channel_id=1, source_target_pairs={{1,0},{2,1},{3,2},{4,3},{5,4},{6,5},{7,6},{8,7},{9,8},{10,9},{11,1... | collective-permute-start | bytes 7556 | tf_op jit(solution)/shard_map/ppermute | solution.py:30
  19.6 61.5 %copy-start.1 = (s32[40,128]{1,0:T(8,128)S(1)}, s32[40,128]{1,0:T(8,128)}, u32[]{:S(2)}) copy-start(s32[40,128]{1,0:T(8,128)} %param.10) | copy-start | bytes 61444
  44.4 26.1 %collective-permute-start.4 = (f32[10,128]{1,0:T(8,128)S(1)}, f32[10,128]{1,0:T(8,128)S(1)}, u32[]{:S(2)}, u32[]{:S(2)}) collective-permute-start(f32[10,128]{1,0:T(8,128)S(1)} %get-tuple-element.279), channel_id=1, source_target_pairs={{0,32},{32,64},{64,96},{96,128},{128,160},{160,192},{192,224},{224... | collective-permute-start | bytes 15368 | tf_op jit(solution)/shard_map/ppermute | solution.py:27
  49.0 21.5 %collective-permute-start.5 = (f32[10,128]{1,0:T(8,128)S(1)}, f32[10,128]{1,0:T(8,128)S(1)}, u32[]{:S(2)}, u32[]{:S(2)}) collective-permute-start(f32[10,128]{1,0:T(8,128)S(1)} %get-tuple-element.280), channel_id=1, source_target_pairs={{32,0},{64,32},{96,64},{128,96},{160,128},{192,160},{224,192},{256... | collective-permute-start | bytes 15368 | tf_op jit(solution)/shard_map/ppermute | solution.py:30
  70.6 8.1 %collective-permute-start.6 = (f32[60,10]{1,0:T(8,128)S(1)}, f32[60,10]{1,0:T(8,128)S(1)}, u32[]{:S(2)}, u32[]{:S(2)}) collective-permute-start(f32[60,10]{1,0:T(8,128)S(1)} %get-tuple-element.275), channel_id=1, source_target_pairs={{0,1},{1,2},{2,3},{3,4},{4,5},{5,6},{6,7},{7,8},{8,9},{9,10},{10,1... | collective-permute-start | bytes 7208 | tf_op jit(solution)/shard_map/ppermute | solution.py:27
  72.6 7.6 %collective-permute-start.7 = (f32[60,10]{1,0:T(8,128)S(1)}, f32[60,10]{1,0:T(8,128)S(1)}, u32[]{:S(2)}, u32[]{:S(2)}) collective-permute-start(f32[60,10]{1,0:T(8,128)S(1)} %get-tuple-element.276), channel_id=1, source_target_pairs={{1,0},{2,1},{3,2},{4,3},{5,4},{6,5},{7,6},{8,7},{9,8},{10,9},{11,1... | collective-permute-start | bytes 7208 | tf_op jit(solution)/shard_map/ppermute | solution.py:30
  88.3 25.5 %collective-permute-start.8 = (f32[10,128]{1,0:T(8,128)S(1)}, f32[10,128]{1,0:T(8,128)S(1)}, u32[]{:S(2)}, u32[]{:S(2)}) collective-permute-start(f32[10,128]{1,0:T(8,128)S(1)} %get-tuple-element.277), channel_id=1, source_target_pairs={{0,32},{32,64},{64,96},{96,128},{128,160},{160,192},{192,224},{224... | collective-permute-start | bytes 15368 | tf_op jit(solution)/shard_map/ppermute | solution.py:27
  92.4 21.5 %collective-permute-start.9 = (f32[10,128]{1,0:T(8,128)S(1)}, f32[10,128]{1,0:T(8,128)S(1)}, u32[]{:S(2)}, u32[]{:S(2)}) collective-permute-start(f32[10,128]{1,0:T(8,128)S(1)} %get-tuple-element.278), channel_id=1, source_target_pairs={{32,0},{64,32},{96,64},{128,96},{160,128},{192,160},{224,192},{256... | collective-permute-start | bytes 15368 | tf_op jit(solution)/shard_map/ppermute | solution.py:30
  114.0 8.1 %collective-permute-start.10 = (f32[60,10]{1,0:T(8,128)S(1)}, f32[60,10]{1,0:T(8,128)S(1)}, u32[]{:S(2)}, u32[]{:S(2)}) collective-permute-start(f32[60,10]{1,0:T(8,128)S(1)} %get-tuple-element.273), channel_id=1, source_target_pairs={{0,1},{1,2},{2,3},{3,4},{4,5},{5,6},{6,7},{7,8},{8,9},{9,10},{10,1... | collective-permute-start | bytes 7208 | tf_op jit(solution)/shard_map/ppermute | solution.py:27
  117.4 6.1 %collective-permute-start.11 = (f32[60,10]{1,0:T(8,128)S(1)}, f32[60,10]{1,0:T(8,128)S(1)}, u32[]{:S(2)}, u32[]{:S(2)}) collective-permute-start(f32[60,10]{1,0:T(8,128)S(1)} %get-tuple-element.274), channel_id=1, source_target_pairs={{1,0},{2,1},{3,2},{4,3},{5,4},{6,5},{7,6},{8,7},{9,8},{10,9},{11,1... | collective-permute-start | bytes 7208 | tf_op jit(solution)/shard_map/ppermute | solution.py:30
  129.1 6.0 %collective-permute-start.12 = (bf16[24,17,128]{2,0,1:T(8,128)(2,1)S(1)}, bf16[24,17,128]{2,0,1:T(8,128)(2,1)S(1)}, u32[]{:S(2)}, u32[]{:S(2)}) collective-permute-start(bf16[24,17,128]{2,0,1:T(8,128)(2,1)S(1)} %get-tuple-element.271), channel_id=1, source_target_pairs={{0,32},{32,64},{64,96},{96,128},{128,160},{160,192},{192,224},{224... | collective-permute-start | bytes 313352 | tf_op jit(solution)/shard_map/ppermute | solution.py:27
  133.8 5.3 %collective-permute-start.13 = (bf16[24,17,128]{2,0,1:T(8,128)(2,1)S(1)}, bf16[24,17,128]{2,0,1:T(8,128)(2,1)S(1)}, u32[]{:S(2)}, u32[]{:S(2)}) collective-permute-start(bf16[24,17,128]{2,0,1:T(8,128)(2,1)S(1)} %get-tuple-element.272), channel_id=1, source_target_pairs={{32,0},{64,32},{96,64},{128,96},{160,128},{192,160},{224,192},{256... | collective-permute-start | bytes 313352 | tf_op jit(solution)/shard_map/ppermute | solution.py:30
  139.3 15.1 %collective-permute-start.14 = (bf16[24,74,17]{2,0,1:T(8,128)(2,1)S(1)}, bf16[24,74,17]{2,0,1:T(8,128)(2,1)S(1)}, u32[]{:S(2)}, u32[]{:S(2)}) collective-permute-start(bf16[24,74,17]{2,0,1:T(8,128)(2,1)S(1)} %get-tuple-element.269), channel_id=1, source_target_pairs={{0,1},{1,2},{2,3},{3,4},{4,5},{5,6},{6,7},{7,8},{8,9},{9,10},{10,1... | collective-permute-start | bytes 181160 | tf_op jit(solution)/shard_map/ppermute | solution.py:27
  143.2 13.0 %collective-permute-start.15 = (bf16[24,74,17]{2,0,1:T(8,128)(2,1)S(1)}, bf16[24,74,17]{2,0,1:T(8,128)(2,1)S(1)}, u32[]{:S(2)}, u32[]{:S(2)}) collective-permute-start(bf16[24,74,17]{2,0,1:T(8,128)(2,1)S(1)} %get-tuple-element.270), channel_id=1, source_target_pairs={{1,0},{2,1},{3,2},{4,3},{5,4},{6,5},{7,6},{8,7},{9,8},{10,9},{11,1... | collective-permute-start | bytes 181160 | tf_op jit(solution)/shard_map/ppermute | solution.py:30
  156.8 161.3 %copy-start = (f32[40,128]{1,0:T(8,128)S(1)}, f32[40,128]{1,0:T(8,128)}, u32[]{:S(2)}) copy-start(f32[40,128]{1,0:T(8,128)} %param.9) | copy-start | bytes 61444
where the time goes:
time: 322 us; the launch traced here: 319 us
  local copies, waits for them, and re-layouts  82.5 us (26%)
  blocking collectives  61 us (19%)
  starting transfers between devices  52.5 us (16%)
  between operations  42.2 us (13%)
  matrix products  40.9 us (13%)
  other arithmetic  22.6 us (7%)
  waiting for transfers between devices  15.3 us (5%)
    psum x4, blocking collectives, one_axis_at_a_time(): value = lax.psum(value, axis)  61 us
    slice x70, local copies, waits for them, and re-layouts, one_row(): mixed[b, :, reach - b:reach - b + out_cols]  55.1 us
    dot_general x35, matrix products, one_row(): jnp.einsum('cb,cyx->byx', row_weights, band, preferred_element_type=jnp.f...  38.7 us
    ppermute x8, starting transfers between devices, with_halo(): lax.ppermute(lax.slice_in_dim(block, block.shape[dim] - width, None, axis...  27.7 us
    ppermute x8, starting transfers between devices, with_halo(): lax.ppermute(lax.slice_in_dim(block, 0, width, axis=dim), axis, backward)  24.8 us
    while x340, local copies, waits for them, and re-layouts  21.4 us
    ppermute x8, waiting for transfers between devices, with_halo(): lax.ppermute(lax.slice_in_dim(block, 0, width, axis=dim), axis, backward)  8.59 us
    ppermute x8, waiting for transfers between devices, with_halo(): lax.ppermute(lax.slice_in_dim(block, block.shape[dim] - width, None, axis...  6.74 us
  transfers between devices with their start and end apart: 16, of which 5 were waited for; matrix products, arithmetic and copies ran while one was open for 2% of the time, Pallas kernels for 0%

commit v1 on v0

v1 whole, which is shorter than its diff:
```python
import functools

import jax
import jax.numpy as jnp
from jax import lax
from jax.experimental import pallas as pl
from jax.experimental.pallas import tpu as pltpu
from jax.sharding import PartitionSpec as P

MESH = pl.DeviceIdType.MESH
F32 = jnp.float32
BF16 = jnp.bfloat16

KERNELS = 12
CHANNELS = 24
TAPS = 35
REACH = 8
LOAD_TAPS = 8
SMOOTH_TAPS = (0.0625, 0.25, 0.375, 0.25, 0.0625)
SHARPNESS = 4.0
THRESHOLD = 0.65
LOADING_GAIN = 0.5

ROWS, COLS = 40, 128
LANES = 256
FIELD_MARGIN = 37
PLANE_MARGIN = 54
PITCH = 40
BAND = 8
DEPTH = 1792
BANDS = 15
FIRST_BAND, LAST_BAND = 2, 11


def lane_index(rows, lanes=LANES):
    return lax.broadcasted_iota(jnp.int32, (rows, lanes), 1)


def row_index(rows, lanes=LANES):
    return lax.broadcasted_iota(jnp.int32, (rows, lanes), 0)


def smooth(ref, start, rows):
    down = sum(SMOOTH_TAPS[a] * ref[pl.ds(start + a - 2, rows), :] for a in range(5))
    total = SMOOTH_TAPS[2] * down
    for b in (0, 1, 3, 4):
        total = total + SMOOTH_TAPS[b] * pltpu.roll(down, (2 - b) % LANES, 1)
    return total


def rows_from(halves, start, rows):
    return jnp.concatenate([halves[i, pl.ds(start, rows), :] for i in range(2)], axis=1)


def build_taps(kernels_ref, flipped, base, taps32, taps, mixer32, mixer):
    flip = (
        lax.broadcasted_iota(jnp.int32, (TAPS, 128), 0) + lax.broadcasted_iota(jnp.int32, (TAPS, 128), 1) == TAPS - 1
    ).astype(BF16)
    for c in range(CHANNELS):
        flipped[c * PITCH : c * PITCH + TAPS, :] = jnp.dot(kernels_ref[c], flip, preferred_element_type=F32)
    lane = lane_index(CHANNELS, 128)
    tiles = [jnp.zeros((CHANNELS, 128), F32) for _ in range(DEPTH // 128)]
    for a in range(TAPS):
        tile, shift = divmod(a * PITCH, 128)
        row = flipped[pl.ds(a, CHANNELS, stride=PITCH), :]
        moved = pltpu.roll(row, shift, 1) if shift else row
        tiles[tile] = tiles[tile] + jnp.where(lane >= shift, moved, 0.0)
        if shift + TAPS > 128:
            tiles[tile + 1] = tiles[tile + 1] + jnp.where(lane < shift, moved, 0.0)
    for i, tile in enumerate(tiles):
        base[:, i * 128 : (i + 1) * 128] = tile
    for y in range(BAND):
        moved = base[...]
        if y:
            moved = pltpu.roll(moved, y * PITCH, 1)
        for i in range(DEPTH // 128):
            taps32[i, pl.ds(y, CHANNELS, stride=BAND), :] = moved[:, i * 128 : (i + 1) * 128]
    joined = jnp.concatenate([taps32[i] for i in range(DEPTH // 128)], axis=1)
    taps[...] = joined.astype(BF16)
    rows = CHANNELS * BAND
    for n in range(6):
        first = (PLANE_MARGIN - 8 * (n + 2)) * PITCH
        low, high = max(first, 0), min(first + 8 * PITCH, DEPTH)
        window = joined[:, low:high]
        if first < 0:
            window = jnp.concatenate([jnp.zeros((rows, -first), F32), window], axis=1)
        if high < first + 8 * PITCH:
            window = jnp.concatenate([window, jnp.zeros((rows, first + 8 * PITCH - high), F32)], axis=1)
        mixer32[n * rows : (n + 1) * rows, 0 : 8 * PITCH] = window
    mixer[...] = mixer32[...].T[0 : 8 * PITCH, :].astype(BF16)


def kernel(
    sizes,
    offsets_ref,
    weights_ref,
    mask_ref,
    target_ref,
    kernels_ref,
    update_ref,
    loss_ref,
    whole,
    edges,
    rims,
    got_whole,
    got_edges,
    got_rims,
    sums_y,
    sums_x,
    flipped,
    base,
    taps32,
    taps,
    mixer32,
    mixer,
    plane,
    wanted,
    patches,
    field,
    buf_a,
    buf_b,
    buf_c,
    halves_b,
    halves_c,
    products,
    mixed,
    send_sem,
    recv_sem,
    sum_send,
    sum_recv,
):
    ny, nx = sizes
    gy, gx = lax.axis_index("gy"), lax.axis_index("gx")

    def at(dy, dx):
        return (lax.rem(gy + (dy % ny), ny), lax.rem(gx + (dx % nx), nx))

    peers = {(dy % ny, dx % nx) for dy in range(-2, 3) for dx in range(-1, 2)}
    peers |= {(d, 0) for d in range(ny)} | {(0, d) for d in range(nx)}
    peers = sorted(peers - {(0, 0)})
    barrier = pltpu.get_barrier_semaphore()
    for dy, dx in peers:
        pl.semaphore_signal(barrier, inc=1, device_id=at(dy, dx), device_id_type=MESH)

    own_plane = mask_ref[...].astype(BF16).astype(F32)
    own_target = target_ref[...].astype(F32)
    lane = lane_index(ROWS, 128)
    whole[0] = own_plane.astype(BF16)
    whole[1] = own_target.astype(BF16)
    left = jnp.where(lane < 64, own_plane, pltpu.roll(own_target, 64, 1))
    right = jnp.where(lane < 64, pltpu.roll(own_plane, 54, 1), pltpu.roll(own_target, 91, 1))
    edges[0] = left.astype(BF16)
    edges[1] = right.astype(BF16)
    for i, value in enumerate((right, own_plane, left)):
        rims[i, 0] = value[24:40, :].astype(BF16)
        rims[i, 1] = value[0:16, :].astype(BF16)

    build_taps(kernels_ref, flipped, base, taps32, taps, mixer32, mixer)

    pl.semaphore_wait(barrier, len(peers))

    copies = []

    def send(source, target, dy, dx):
        slot = len(copies)
        copies.append(
            pltpu.make_async_remote_copy(
                src_ref=source,
                dst_ref=target,
                send_sem=send_sem.at[slot],
                recv_sem=recv_sem.at[slot],
                device_id=at(dy, dx),
                device_id_type=MESH,
            )
        )
        copies[-1].start()

    for dx in (1, -1):
        side = 1 if dx == 1 else 0
        for dy in (-1, 0, 1):
            send(edges.at[side], got_edges.at[0 if dx == 1 else 1, 1 - dy], dy, dx)
    for dx in (1, -1, 0):
        for dy in (2, -2):
            end = 0 if dy == 2 else 1
            send(rims.at[1 - dx, end], got_rims.at[1 - dx, end], dy, dx)
    for dy in (1, -1):
        send(whole, got_whole.at[0 if dy == 1 else 1], dy, 0)
    for copy in copies:
        copy.wait()

    first_row = gy * ROWS
    first_col = gx * COLS
    total_rows, total_cols = ny * ROWS, nx * COLS

    def framed(row, rows, middle, west, east):
        n = lane_index(rows, 128)
        moved = pltpu.roll(middle, PLANE_MARGIN, 1)
        low = jnp.where(n < PLANE_MARGIN, west, moved)
        high = jnp.where(n < PLANE_MARGIN, moved, jnp.where(n < 2 * PLANE_MARGIN, pltpu.roll(east, 54, 1), 0.0))
        value = jnp.concatenate([low, high], axis=1)
        y = first_row - PLANE_MARGIN - 2 + row + row_index(rows)
        x = first_col - PLANE_MARGIN + lane_index(rows)
        inside = (y >= 0) & (y < total_rows) & (x >= 0) & (x < total_cols)
        plane[row : row + rows, :] = pltpu.roll(jnp.where(inside, value, 0.0), LANES - TAPS + 1, 1)

    def wide(value):
        return value.astype(F32)

    framed(0, 16, wide(got_rims[1, 0]), wide(got_rims[0, 0]), wide(got_rims[2, 0]))
    framed(16, 40, wide(got_whole[0, 0]), wide(got_edges[0, 0]), wide(got_edges[1, 0]))
    framed(56, 40, own_plane, wide(got_edges[0, 1]), wide(got_edges[1, 1]))
    framed(96, 40, wide(got_whole[1, 0]), wide(got_edges[0, 2]), wide(got_edges[1, 2]))
    framed(136, 16, wide(got_rims[1, 1]), wide(got_rims[0, 1]), wide(got_rims[2, 1]))
    plane[152:160, :] = jnp.zeros((8, LANES), F32)

    def framed_target(row, middle, west, east):
        n = lane_index(ROWS, 128)
        moved = pltpu.roll(middle, FIELD_MARGIN, 1)
        wanted[row : row + ROWS, 0:128] = jnp.where(n < FIELD_MARGIN, pltpu.roll(west, 74, 1), moved)
        wanted[row : row + ROWS, 128:256] = jnp.where(n < FIELD_MARGIN, moved, pltpu.roll(east, 101, 1))

    framed_target(0, wide(got_whole[0, 1]), wide(got_edges[0, 0]), wide(got_edges[1, 0]))
    framed_target(40, own_target, wide(got_edges[0, 1]), wide(got_edges[1, 1]))
    framed_target(80, wide(got_whole[1, 1]), wide(got_edges[0, 2]), wide(got_edges[1, 2]))

    def spread(step, carry):
        pieces = []
        for i in range(2):
            row = plane[pl.ds(step * 2 + i + 2, 1), :]
            row = jnp.broadcast_to(row, (PITCH, LANES))
            pieces.append(pltpu.roll(row, 0, 1, stride=1, stride_axis=0))
        value = jnp.concatenate(pieces, axis=0).astype(BF16)
        patches[pl.ds(pl.multiple_of(step * 2 * PITCH, 2 * PITCH), 2 * PITCH), :] = value
        return carry

    lax.fori_loop(0, 79, spread, 0)

    def inside_field(start, rows):
        y = first_row - FIELD_MARGIN + start + row_index(rows)
        x = first_col - FIELD_MARGIN + lane_index(rows)
        return (y >= 0) & (y < total_rows) & (x >= 0) & (x < total_cols)

    for ref in (buf_a, buf_b, buf_c):
        ref[0:8, :] = jnp.zeros((8, LANES), F32)
        ref[8 + BANDS * BAND :, :] = jnp.zeros((8, LANES), F32)

    def band(i, carry):
        rows = pl.ds(pl.multiple_of(i * BAND * PITCH, BAND * PITCH), DEPTH)
        value = jnp.dot(taps[...], patches[rows, :], preferred_element_type=F32)
        value = value.reshape(CHANNELS, BAND, LANES)
        start = pl.multiple_of(i * BAND, BAND)
        field[:, pl.ds(start, BAND), :] = value
        intensity = jnp.sum(value * value, axis=0) / KERNELS
        buf_a[pl.ds(start + 8, BAND), :] = jnp.where(inside_field(start, BAND), intensity, 0.0)
        return carry

    lax.fori_loop(0, BANDS, band, 0)

    dense = smooth(buf_a, 8, 120)
    develop = jnp.where(inside_field(0, 120), jax.nn.sigmoid(SHARPNESS * (dense - THRESHOLD)), 0.0)
    buf_b[8:128, :] = develop
    for i in range(2):
        halves_b[i, 8:128, :] = develop[:, i * 128 : (i + 1) * 128]
        halves_b[i, 0:8, :] = jnp.zeros((8, 128), F32)
        halves_b[i, 128:136, :] = jnp.zeros((8, 128), F32)

    loading = jnp.zeros((104, LANES), F32)
    for j in range(LOAD_TAPS):
        part = rows_from(halves_b, 16 + offsets_ref[j, 0], 104)
        loading = loading + weights_ref[j] * pltpu.roll(part, lax.rem(LANES - offsets_ref[j, 1], LANES), 1)
    printed = buf_b[16:120, :] - LOADING_GAIN / LOAD_TAPS * loading
    y = first_row - FIELD_MARGIN + 8 + row_index(104)
    x = first_col - FIELD_MARGIN + lane_index(104)
    weight = (1.0 + 2.0 * y.astype(F32) / total_rows) * (1.0 + 2.0 * x.astype(F32) / total_cols)
    diff = printed - wanted[11:115, :]
    own = (y >= first_row) & (y < first_row + ROWS) & (x >= first_col) & (x < first_col + COLS)
    loss = jnp.sum(jnp.where(own, weight * diff * diff, 0.0), axis=0, keepdims=True)
    resid = jnp.where(inside_field(8, 104), 2.0 * weight * diff, 0.0)
    buf_c[16:120, :] = resid
    for i in range(2):
        halves_c[i, 16:120, :] = resid[:, i * 128 : (i + 1) * 128]

    back = jnp.zeros((88, LANES), F32)
    for j in range(LOAD_TAPS):
        part = rows_from(halves_c, 24 - offsets_ref[j, 0], 88)
        back = back + weights_ref[j] * pltpu.roll(part, lax.rem(LANES + offsets_ref[j, 1], LANES), 1)
    slope = buf_c[24:112, :] - LOADING_GAIN / LOAD_TAPS * back
    nearby = buf_b[24:112, :]
    buf_a[24:112, :] = slope * SHARPNESS * nearby * (1.0 - nearby)
    pull = smooth(buf_a, 24, 80)
    buf_b[24:104, :] = jnp.where(inside_field(16, 80), pull, 0.0)

    def weigh(i, carry):
        start = pl.multiple_of((i + FIRST_BAND) * BAND, BAND)
        value = 2.0 * field[:, pl.ds(start, BAND), :] * buf_b[pl.ds(start + 8, BAND), :][None] / KERNELS
        rows = pl.ds(pl.multiple_of(i * CHANNELS * BAND, CHANNELS * BAND), CHANNELS * BAND)
        products[rows, :] = value.reshape(CHANNELS * BAND, LANES).astype(BF16)
        return carry

    lax.fori_loop(0, LAST_BAND - FIRST_BAND + 1, weigh, 0)

    def mix(g, carry):
        rows = pl.ds(pl.multiple_of(g * CHANNELS * BAND, CHANNELS * BAND), 6 * CHANNELS * BAND)
        value = jnp.dot(mixer[...], products[rows, :], preferred_element_type=F32)
        for i in range(2):
            mixed[i, pl.ds(pl.multiple_of(g * 8 * PITCH, 8 * PITCH), 8 * PITCH), :] = value[:, i * 128 : (i + 1) * 128]
        return carry

    lax.fori_loop(0, ROWS // 8, mix, 0)

    gradient = jnp.zeros((ROWS, 128), F32)
    for t in range(TAPS):
        part = jnp.concatenate([mixed[i, pl.ds(t, ROWS, stride=PITCH), :] for i in range(2)], axis=1)
        gradient = gradient + pltpu.roll(part, 236 - t, 1)[:, 0:128]

    def gather(sums, axis_size, me, number):
        out = []
        for d in range(1, axis_size):
            peer = lax.rem(me + d, axis_size)
            out.append(
                pltpu.make_async_remote_copy(
                    src_ref=sums.at[me],
                    dst_ref=sums.at[me],
                    send_sem=sum_send.at[number, d],
                    recv_sem=sum_recv.at[number, d],
                    device_id=(peer, gx) if number == 0 else (gy, peer),
                    device_id_type=MESH,
                )
            )
            out[-1].start()
        for copy in out:
            copy.wait()

    square = jnp.sum(gradient * gradient, axis=0, keepdims=True)
    sums_y[gy, 0:1, :] = loss[:, 0:128] + loss[:, 128:256]
    sums_y[gy, 1:2, :] = square
    gather(sums_y, ny, gy, 0)
    sums_x[gx] = jnp.sum(sums_y[...], axis=0)
    gather(sums_x, nx, gx, 1)
    totals = jnp.sum(jnp.sum(sums_x[...], axis=0), axis=1, keepdims=True)
    loss_ref[...] = totals[0:1, :]
    scale = jnp.sqrt(totals[1:2, :] / (total_rows * total_cols) + 1e-06)
    update_ref[...] = mask_ref[...] - gradient / scale


def solution(mesh):
    ny, nx = mesh.shape["gy"], mesh.shape["gx"]
    vmem = pl.BlockSpec(memory_space=pltpu.VMEM)
    smem = pl.BlockSpec(memory_space=pltpu.SMEM)
    rows = CHANNELS * BAND

    def step(mask, target, kernels, offsets, load_weights):
        update, loss = pl.pallas_call(
            functools.partial(kernel, (ny, nx)),
            out_shape=(
                jax.ShapeDtypeStruct((ROWS, COLS), F32),
                jax.ShapeDtypeStruct((1, 1), F32),
            ),
            in_specs=[smem, smem, vmem, vmem, vmem],
            out_specs=(vmem, vmem),
            scratch_shapes=[
                pltpu.VMEM((2, ROWS, COLS), BF16),
                pltpu.VMEM((2, ROWS, COLS), BF16),
                pltpu.VMEM((3, 2, 16, COLS), BF16),
                pltpu.VMEM((2, 2, ROWS, COLS), BF16),
                pltpu.VMEM((2, 3, ROWS, COLS), BF16),
                pltpu.VMEM((3, 2, 16, COLS), BF16),
                pltpu.VMEM((ny, 2, 128), F32),
                pltpu.VMEM((nx, 2, 128), F32),
                pltpu.VMEM((CHANNELS * PITCH, 128), F32),
                pltpu.VMEM((CHANNELS, DEPTH), F32),
                pltpu.VMEM((DEPTH // 128, rows, 128), F32),
                pltpu.VMEM((rows, DEPTH), BF16),
                pltpu.VMEM((6 * rows, 384), F32),
                pltpu.VMEM((8 * PITCH, 6 * rows), BF16),
                pltpu.VMEM((160, LANES), F32),
                pltpu.VMEM((120, LANES), F32),
                pltpu.VMEM((6320, LANES), BF16),
                pltpu.VMEM((CHANNELS, BANDS * BAND, LANES), F32),
                pltpu.VMEM((136, LANES), F32),
                pltpu.VMEM((136, LANES), F32),
                pltpu.VMEM((136, LANES), F32),
                pltpu.VMEM((2, 136, 128), F32),
                pltpu.VMEM((2, 136, 128), F32),
                pltpu.VMEM((10 * rows, LANES), BF16),
                pltpu.VMEM((2, ROWS * PITCH, 128), F32),
                pltpu.SemaphoreType.DMA((14,)),
                pltpu.SemaphoreType.DMA((14,)),
                pltpu.SemaphoreType.DMA((2, 32)),
                pltpu.SemaphoreType.DMA((2, 32)),
            ],
            compiler_params=pltpu.CompilerParams(collective_id=0, has_side_effects=True),
        )(offsets, load_weights, mask, target, kernels)
        return update, loss[0, 0]

    placed = (P("gy", "gx"), P("gy", "gx"), P(), P(), P())
    return jax.shard_map(step, mesh=mesh, in_specs=placed, out_specs=(P("gy", "gx"), P()), check_vma=False)
```

time: 322 us -> 56.5 us (0.18)
  the two profiles are of different devices: /device:TPU:16 before, /device:TPU:1 now
where the time goes in v1:
time: 56.5 us; the launch traced here: 56.3 us
  Pallas kernels  49.6 us (88%)
  local copies, waits for them, and re-layouts  4.34 us (8%)
  between operations  2.31 us (4%)
    pallas_call x1, Pallas kernels, step(): pl.pallas_call(functools.partial(kernel, (ny, nx)), out_shape=(jax.ShapeD...  49.6 us
    unnamed x3, local copies, waits for them, and re-layouts  4.34 us

profile of v1, /device:TPU:1, one launch (start us, length us, event | category | flops | bytes accessed | tf_op | source)
XLA Modules:
  0.0 56.3 jit_solution(2110208065130931287)
XLA Ops:
  0.6 1.3 %copy.7.offsets_ref = s32[8,2]{1,0:T(8,128)} copy(s32[8,2]{0,1:T(2,128)} %param.8) | data formatting | bytes 128 | tf_op args[3]
  2.0 1.7 %copy.8.kernels_ref = bf16[24,35,35]{2,1,0:T(8,128)(2,1)} copy(bf16[24,35,35]{2,0,1:T(8,128)(2,1)} %param.7) | data formatting | bytes 117600 | tf_op args[2]
  3.6 49.6 %shard_map.68 = (f32[40,128]{1,0:T(8,128)}, f32[1,1]{1,0:T(1,128)}) custom-call(s32[8,2]{1,0:T(8,128)} %copy.7.offsets_ref, f32[8]{0:T(128)} %weights_ref.1, f32[40,128]{1,0:T(8,128)} %mask_ref.1, s32[40,128]{1,0:T(8,128)} %target_ref.1, bf16[24,35,35]{2,1,0:T(8,128)(2,1)} %copy.8.kernels_ref), custom_call_target="tpu_custom_call" | custom-call | tf_op jit(solution)/shard_map/pallas_call | solution.py:353
  53.3 1.3 %copy.11 = f32[40,128]{1,0:T(8,128)} copy(f32[40,128]{1,0:T(8,128)} %get-tuple-element.8) | data formatting | bytes 40960

commit v2 on v1

--- a/solution.py
+++ b/solution.py
@@ -25,9 +25,9 @@
 LANES = 256
 FIELD_MARGIN = 37
 PLANE_MARGIN = 54
-PITCH = 40
+PITCH = 36
 BAND = 8
-DEPTH = 1792
+DEPTH = 1536
 BANDS = 15
 FIRST_BAND, LAST_BAND = 2, 11
 
@@ -52,31 +52,30 @@
     return jnp.concatenate([halves[i, pl.ds(start, rows), :] for i in range(2)], axis=1)
 
 
-def build_taps(kernels_ref, flipped, base, taps32, taps, mixer32, mixer):
+def build_taps(kernels_ref, taps32, taps):
     flip = (
         lax.broadcasted_iota(jnp.int32, (TAPS, 128), 0) + lax.broadcasted_iota(jnp.int32, (TAPS, 128), 1) == TAPS - 1
     ).astype(BF16)
-    for c in range(CHANNELS):
-        flipped[c * PITCH : c * PITCH + TAPS, :] = jnp.dot(kernels_ref[c], flip, preferred_element_type=F32)
     lane = lane_index(CHANNELS, 128)
     tiles = [jnp.zeros((CHANNELS, 128), F32) for _ in range(DEPTH // 128)]
     for a in range(TAPS):
         tile, shift = divmod(a * PITCH, 128)
-        row = flipped[pl.ds(a, CHANNELS, stride=PITCH), :]
+        row = jnp.dot(kernels_ref[a], flip, preferred_element_type=F32)
         moved = pltpu.roll(row, shift, 1) if shift else row
         tiles[tile] = tiles[tile] + jnp.where(lane >= shift, moved, 0.0)
         if shift + TAPS > 128:
             tiles[tile + 1] = tiles[tile + 1] + jnp.where(lane < shift, moved, 0.0)
-    for i, tile in enumerate(tiles):
-        base[:, i * 128 : (i + 1) * 128] = tile
+    base = jnp.concatenate(tiles, axis=1)
     for y in range(BAND):
-        moved = base[...]
-        if y:
-            moved = pltpu.roll(moved, y * PITCH, 1)
+        moved = pltpu.roll(base, y * PITCH, 1) if y else base
         for i in range(DEPTH // 128):
             taps32[i, pl.ds(y, CHANNELS, stride=BAND), :] = moved[:, i * 128 : (i + 1) * 128]
+    for i in range(DEPTH // 128):
+        taps[:, i * 128 : (i + 1) * 128] = taps32[i].astype(BF16)
+
+
+def build_mixer(taps32, mixer32, mixer):
     joined = jnp.concatenate([taps32[i] for i in range(DEPTH // 128)], axis=1)
-    taps[...] = joined.astype(BF16)
     rows = CHANNELS * BAND
     for n in range(6):
         first = (PLANE_MARGIN - 8 * (n + 2)) * PITCH
@@ -92,13 +91,19 @@
 
 def kernel(
     sizes,
+    offsets_hbm,
+    weights_hbm,
+    mask_hbm,
+    target_hbm,
+    kernels_hbm,
+    update_ref,
+    loss_ref,
     offsets_ref,
     weights_ref,
     mask_ref,
     target_ref,
     kernels_ref,
-    update_ref,
-    loss_ref,
+    input_sem,
     whole,
     edges,
     rims,
@@ -107,8 +112,6 @@
     got_rims,
     sums_y,
     sums_x,
-    flipped,
-    base,
     taps32,
     taps,
     mixer32,
@@ -142,6 +145,23 @@
     for dy, dx in peers:
         pl.semaphore_signal(barrier, inc=1, device_id=at(dy, dx), device_id_type=MESH)
 
+    inputs = [
+        pltpu.make_async_copy(source, target, input_sem.at[i])
+        for i, (source, target) in enumerate(
+            (
+                (mask_hbm, mask_ref),
+                (target_hbm, target_ref),
+                (kernels_hbm, kernels_ref),
+                (offsets_hbm, offsets_ref),
+                (weights_hbm, weights_ref),
+            )
+        )
+    ]
+    for copy in inputs:
+        copy.start()
+    inputs[0].wait()
+    inputs[1].wait()
+
     own_plane = mask_ref[...].astype(BF16).astype(F32)
     own_target = target_ref[...].astype(F32)
     lane = lane_index(ROWS, 128)
@@ -155,7 +175,8 @@
         rims[i, 0] = value[24:40, :].astype(BF16)
         rims[i, 1] = value[0:16, :].astype(BF16)
 
-    build_taps(kernels_ref, flipped, base, taps32, taps, mixer32, mixer)
+    inputs[2].wait()
+    build_taps(kernels_ref, taps32, taps)
 
     pl.semaphore_wait(barrier, len(peers))
 
@@ -185,6 +206,13 @@
             send(rims.at[1 - dx, end], got_rims.at[1 - dx, end], dy, dx)
     for dy in (1, -1):
         send(whole, got_whole.at[0 if dy == 1 else 1], dy, 0)
+    build_mixer(taps32, mixer32, mixer)
+    inputs[3].wait()
+    inputs[4].wait()
+    for ref in (buf_a, buf_b, buf_c):
+        ref[0:8, :] = jnp.zeros((8, LANES), F32)
+        ref[8 + BANDS * BAND :, :] = jnp.zeros((8, LANES), F32)
+    patches[152 * PITCH :, :] = jnp.zeros((96, LANES), BF16)
     for copy in copies:
         copy.wait()
 
@@ -201,7 +229,7 @@
         y = first_row - PLANE_MARGIN - 2 + row + row_index(rows)
         x = first_col - PLANE_MARGIN + lane_index(rows)
         inside = (y >= 0) & (y < total_rows) & (x >= 0) & (x < total_cols)
-        plane[row : row + rows, :] = pltpu.roll(jnp.where(inside, value, 0.0), LANES - TAPS + 1, 1)
+        plane[row : row + rows, :] = pltpu.roll(jnp.where(inside, value, 0.0), LANES - TAPS + 1 - 4, 1)
 
     def wide(value):
         return value.astype(F32)
@@ -223,38 +251,41 @@
     framed_target(40, own_target, wide(got_edges[0, 1]), wide(got_edges[1, 1]))
     framed_target(80, wide(got_whole[1, 1]), wide(got_edges[0, 2]), wide(got_edges[1, 2]))
 
-    def spread(step, carry):
-        pieces = []
-        for i in range(2):
-            row = plane[pl.ds(step * 2 + i + 2, 1), :]
-            row = jnp.broadcast_to(row, (PITCH, LANES))
-            pieces.append(pltpu.roll(row, 0, 1, stride=1, stride_axis=0))
-        value = jnp.concatenate(pieces, axis=0).astype(BF16)
-        patches[pl.ds(pl.multiple_of(step * 2 * PITCH, 2 * PITCH), 2 * PITCH), :] = value
-        return carry
-
-    lax.fori_loop(0, 79, spread, 0)
+    n8 = row_index(8)
+
+    def spread(chunk):
+        for v in range(chunk * 8, chunk * 8 + 8, 4):
+            pieces = []
+            for u in (v, v + 2):
+                even = jnp.broadcast_to(plane[u + 2 : u + 3, :], (40, LANES))
+                odd = jnp.broadcast_to(plane[u + 3 : u + 4, :], (40, LANES))
+                even = pltpu.roll(even, 4, 1, stride=1, stride_axis=0)
+                odd = pltpu.roll(odd, 0, 1, stride=1, stride_axis=0)
+                pieces += [even[0:32], jnp.where(n8 < 4, even[32:40], odd[0:8]), odd[8:40]]
+            patches[v * PITCH : (v + 4) * PITCH, :] = jnp.concatenate(pieces, axis=0).astype(BF16)
+
+    for chunk in range(6):
+        spread(chunk)
 
     def inside_field(start, rows):
         y = first_row - FIELD_MARGIN + start + row_index(rows)
         x = first_col - FIELD_MARGIN + lane_index(rows)
         return (y >= 0) & (y < total_rows) & (x >= 0) & (x < total_cols)
 
-    for ref in (buf_a, buf_b, buf_c):
-        ref[0:8, :] = jnp.zeros((8, LANES), F32)
-        ref[8 + BANDS * BAND :, :] = jnp.zeros((8, LANES), F32)
-
-    def band(i, carry):
-        rows = pl.ds(pl.multiple_of(i * BAND * PITCH, BAND * PITCH), DEPTH)
-        value = jnp.dot(taps[...], patches[rows, :], preferred_element_type=F32)
+    def band(i):
+        first = i * BAND * PITCH
+        value = jnp.dot(taps[...], patches[first : first + DEPTH, :], preferred_element_type=F32)
         value = value.reshape(CHANNELS, BAND, LANES)
-        start = pl.multiple_of(i * BAND, BAND)
-        field[:, pl.ds(start, BAND), :] = value
+        start = i * BAND
+        if FIRST_BAND <= i <= LAST_BAND:
+            field[:, start : start + BAND, :] = value
         intensity = jnp.sum(value * value, axis=0) / KERNELS
-        buf_a[pl.ds(start + 8, BAND), :] = jnp.where(inside_field(start, BAND), intensity, 0.0)
-        return carry
-
-    lax.fori_loop(0, BANDS, band, 0)
+        buf_a[start + 8 : start + 8 + BAND, :] = jnp.where(inside_field(start, BAND), intensity, 0.0)
+
+    for i in range(BANDS):
+        if i + 6 < 19:
+            spread(i + 6)
+        band(i)
 
     dense = smooth(buf_a, 8, 120)
     develop = jnp.where(inside_field(0, 120), jax.nn.sigmoid(SHARPNESS * (dense - THRESHOLD)), 0.0)
@@ -266,8 +297,8 @@
 
     loading = jnp.zeros((104, LANES), F32)
     for j in range(LOAD_TAPS):
-        part = rows_from(halves_b, 16 + offsets_ref[j, 0], 104)
-        loading = loading + weights_ref[j] * pltpu.roll(part, lax.rem(LANES - offsets_ref[j, 1], LANES), 1)
+        part = rows_from(halves_b, 16 + offsets_ref[0, j], 104)
+        loading = loading + weights_ref[j] * pltpu.roll(part, lax.rem(LANES - offsets_ref[1, j], LANES), 1)
     printed = buf_b[16:120, :] - LOADING_GAIN / LOAD_TAPS * loading
     y = first_row - FIELD_MARGIN + 8 + row_index(104)
     x = first_col - FIELD_MARGIN + lane_index(104)
@@ -282,8 +313,8 @@
 
     back = jnp.zeros((88, LANES), F32)
     for j in range(LOAD_TAPS):
-        part = rows_from(halves_c, 24 - offsets_ref[j, 0], 88)
-        back = back + weights_ref[j] * pltpu.roll(part, lax.rem(LANES + offsets_ref[j, 1], LANES), 1)
+        part = rows_from(halves_c, 24 - offsets_ref[0, j], 88)
+        back = back + weights_ref[j] * pltpu.roll(part, lax.rem(LANES + offsets_ref[1, j], LANES), 1)
     slope = buf_c[24:112, :] - LOADING_GAIN / LOAD_TAPS * back
     nearby = buf_b[24:112, :]
     buf_a[24:112, :] = slope * SHARPNESS * nearby * (1.0 - nearby)
@@ -346,7 +377,6 @@
 def solution(mesh):
     ny, nx = mesh.shape["gy"], mesh.shape["gx"]
     vmem = pl.BlockSpec(memory_space=pltpu.VMEM)
-    smem = pl.BlockSpec(memory_space=pltpu.SMEM)
     rows = CHANNELS * BAND
 
     def step(mask, target, kernels, offsets, load_weights):
@@ -356,9 +386,15 @@
                 jax.ShapeDtypeStruct((ROWS, COLS), F32),
                 jax.ShapeDtypeStruct((1, 1), F32),
             ),
-            in_specs=[smem, smem, vmem, vmem, vmem],
+            in_specs=[pl.BlockSpec(memory_space=pl.ANY)] * 5,
             out_specs=(vmem, vmem),
             scratch_shapes=[
+                pltpu.SMEM((2, LOAD_TAPS), jnp.int32),
+                pltpu.SMEM((LOAD_TAPS,), F32),
+                pltpu.VMEM((ROWS, COLS), F32),
+                pltpu.VMEM((ROWS, COLS), jnp.int32),
+                pltpu.VMEM((TAPS, CHANNELS, TAPS), BF16),
+                pltpu.SemaphoreType.DMA((5,)),
                 pltpu.VMEM((2, ROWS, COLS), BF16),
                 pltpu.VMEM((2, ROWS, COLS), BF16),
                 pltpu.VMEM((3, 2, 16, COLS), BF16),
@@ -367,15 +403,13 @@
                 pltpu.VMEM((3, 2, 16, COLS), BF16),
                 pltpu.VMEM((ny, 2, 128), F32),
                 pltpu.VMEM((nx, 2, 128), F32),
-                pltpu.VMEM((CHANNELS * PITCH, 128), F32),
-                pltpu.VMEM((CHANNELS, DEPTH), F32),
                 pltpu.VMEM((DEPTH // 128, rows, 128), F32),
                 pltpu.VMEM((rows, DEPTH), BF16),
                 pltpu.VMEM((6 * rows, 384), F32),
                 pltpu.VMEM((8 * PITCH, 6 * rows), BF16),
                 pltpu.VMEM((160, LANES), F32),
                 pltpu.VMEM((120, LANES), F32),
-                pltpu.VMEM((6320, LANES), BF16),
+                pltpu.VMEM((152 * PITCH + 96, LANES), BF16),
                 pltpu.VMEM((CHANNELS, BANDS * BAND, LANES), F32),
                 pltpu.VMEM((136, LANES), F32),
                 pltpu.VMEM((136, LANES), F32),
@@ -390,7 +424,7 @@
                 pltpu.SemaphoreType.DMA((2, 32)),
             ],
             compiler_params=pltpu.CompilerParams(collective_id=0, has_side_effects=True),
-        )(offsets, load_weights, mask, target, kernels)
+        )(offsets.T, load_weights, mask, target, kernels.transpose(1, 0, 2))
         return update, loss[0, 0]
 
     placed = (P("gy", "gx"), P("gy", "gx"), P(), P(), P())

time: 56.5 us -> 43 us (0.76)
  Pallas kernels: 49.6 us -> 39 us
  local copies, waits for them, and re-layouts: 4.34 us -> 1.34 us
    pallas_call x1, Pallas kernels: 49.6 us -> 39 us  [step(): pl.pallas_call(functools.partial(kernel, (ny, nx)), out_shape=(jax.ShapeD...]
    unnamed x3 -> x1, local copies, waits for them, and re-layouts: 4.34 us -> 1.34 us
where the time goes in v2:
time: 43 us; the launch traced here: 42.8 us
  Pallas kernels  39 us (91%)
  between operations  2.4 us (6%)
  local copies, waits for them, and re-layouts  1.34 us (3%)
    pallas_call x1, Pallas kernels, step(): pl.pallas_call(functools.partial(kernel, (ny, nx)), out_shape=(jax.ShapeD...  39 us
    unnamed x1, local copies, waits for them, and re-layouts  1.34 us

profile of v2, /device:TPU:1, one launch (start us, length us, event | category | flops | bytes accessed | tf_op | source)
XLA Modules:
  0.0 42.8 jit_solution(11585691283738545700)
XLA Ops:
  0.6 39.0 %shard_map.68 = (f32[40,128]{1,0:T(8,128)}, f32[1,1]{1,0:T(1,128)}) custom-call(s32[2,8]{1,0:T(2,128)} %bitcast.4, f32[8]{0:T(128)} %weights_hbm.1, f32[40,128]{1,0:T(8,128)} %mask_hbm.1, s32[40,128]{1,0:T(8,128)} %target_hbm.1, bf16[35,24,35]{2,1,0:T(8,128)(2,1)} %bitcast.3), custom_call_target="tpu_custom_call" | custom-call | tf_op jit(solution)/shard_map/pallas_call | solution.py:383
  39.7 1.3 %copy.9 = f32[40,128]{1,0:T(8,128)} copy(f32[40,128]{1,0:T(8,128)} %get-tuple-element.8) | data formatting | bytes 40960

commit v3 on v2

--- a/solution.py
+++ b/solution.py
@@ -96,13 +96,14 @@
     mask_hbm,
     target_hbm,
     kernels_hbm,
-    update_ref,
-    loss_ref,
+    gradient_hbm,
+    sums_ref,
     offsets_ref,
     weights_ref,
     mask_ref,
     target_ref,
     kernels_ref,
+    gradient_ref,
     input_sem,
     whole,
     edges,
@@ -131,19 +132,13 @@
     recv_sem,
     sum_send,
     sum_recv,
+    known,
 ):
     ny, nx = sizes
     gy, gx = lax.axis_index("gy"), lax.axis_index("gx")
 
     def at(dy, dx):
         return (lax.rem(gy + (dy % ny), ny), lax.rem(gx + (dx % nx), nx))
-
-    peers = {(dy % ny, dx % nx) for dy in range(-2, 3) for dx in range(-1, 2)}
-    peers |= {(d, 0) for d in range(ny)} | {(0, d) for d in range(nx)}
-    peers = sorted(peers - {(0, 0)})
-    barrier = pltpu.get_barrier_semaphore()
-    for dy, dx in peers:
-        pl.semaphore_signal(barrier, inc=1, device_id=at(dy, dx), device_id_type=MESH)
 
     inputs = [
         pltpu.make_async_copy(source, target, input_sem.at[i])
@@ -159,6 +154,30 @@
     ]
     for copy in inputs:
         copy.start()
+    peers = sorted({(dy % ny, dx % nx) for dy in range(-2, 3) for dx in range(-1, 2)} - {(0, 0)})
+    barrier = pltpu.get_barrier_semaphore()
+    for dy, dx in peers:
+        pl.semaphore_signal(barrier, inc=1, device_id=at(dy, dx), device_id_type=MESH)
+
+    rounds_y = [r for r in (2, 4, 8) if 2 * r < ny]
+    rounds_x = [r for r in (1, 2, 4, 8) if 2 * r < nx]
+
+    def tell(number):
+        for along_x, rounds in ((0, rounds_y), (1, rounds_x)):
+            if number < len(rounds):
+                for r in (rounds[number], -rounds[number]):
+                    pl.semaphore_signal(
+                        known.at[along_x, number],
+                        inc=1,
+                        device_id=at(0, r) if along_x else at(r, 0),
+                        device_id_type=MESH,
+                    )
+
+    def learn(number):
+        for along_x, rounds in ((0, rounds_y), (1, rounds_x)):
+            if number < len(rounds):
+                pl.semaphore_wait(known.at[along_x, number], 2)
+
     inputs[0].wait()
     inputs[1].wait()
 
@@ -175,46 +194,48 @@
         rims[i, 0] = value[24:40, :].astype(BF16)
         rims[i, 1] = value[0:16, :].astype(BF16)
 
-    inputs[2].wait()
-    build_taps(kernels_ref, taps32, taps)
-
     pl.semaphore_wait(barrier, len(peers))
 
-    copies = []
-
-    def send(source, target, dy, dx):
-        slot = len(copies)
-        copies.append(
-            pltpu.make_async_remote_copy(
-                src_ref=source,
-                dst_ref=target,
-                send_sem=send_sem.at[slot],
-                recv_sem=recv_sem.at[slot],
-                device_id=at(dy, dx),
-                device_id_type=MESH,
-            )
-        )
-        copies[-1].start()
+    def send(kind, source, target, dy, dx):
+        pltpu.make_async_remote_copy(
+            src_ref=source,
+            dst_ref=target,
+            send_sem=send_sem.at[kind],
+            recv_sem=recv_sem.at[kind],
+            device_id=at(dy, dx),
+            device_id_type=MESH,
+        ).start()
+
+    def wait_all(ref, sent, received):
+        for sem in (sent, received):
+            pltpu.make_async_copy(ref, ref, sem).wait()
 
     for dx in (1, -1):
         side = 1 if dx == 1 else 0
         for dy in (-1, 0, 1):
-            send(edges.at[side], got_edges.at[0 if dx == 1 else 1, 1 - dy], dy, dx)
+            send(0, edges.at[side], got_edges.at[0 if dx == 1 else 1, 1 - dy], dy, dx)
     for dx in (1, -1, 0):
         for dy in (2, -2):
             end = 0 if dy == 2 else 1
-            send(rims.at[1 - dx, end], got_rims.at[1 - dx, end], dy, dx)
+            send(1, rims.at[1 - dx, end], got_rims.at[1 - dx, end], dy, dx)
     for dy in (1, -1):
-        send(whole, got_whole.at[0 if dy == 1 else 1], dy, 0)
+        send(2, whole, got_whole.at[0 if dy == 1 else 1], dy, 0)
+    tell(0)
+    inputs[2].wait()
+    build_taps(kernels_ref, taps32, taps)
+    learn(0)
+    tell(1)
     build_mixer(taps32, mixer32, mixer)
+    learn(1)
+    tell(2)
     inputs[3].wait()
     inputs[4].wait()
     for ref in (buf_a, buf_b, buf_c):
         ref[0:8, :] = jnp.zeros((8, LANES), F32)
         ref[8 + BANDS * BAND :, :] = jnp.zeros((8, LANES), F32)
     patches[152 * PITCH :, :] = jnp.zeros((96, LANES), BF16)
-    for copy in copies:
-        copy.wait()
+    for kind, ref in enumerate((got_edges, got_rims, got_whole)):
+        wait_all(ref, send_sem.at[kind], recv_sem.at[kind])
 
     first_row = gy * ROWS
     first_col = gx * COLS
@@ -286,6 +307,9 @@
         if i + 6 < 19:
             spread(i + 6)
         band(i)
+        if i == 9:
+            learn(2)
+            tell(3)
 
     dense = smooth(buf_a, 8, 120)
     develop = jnp.where(inside_field(0, 120), jax.nn.sigmoid(SHARPNESS * (dense - THRESHOLD)), 0.0)
@@ -321,57 +345,84 @@
     pull = smooth(buf_a, 24, 80)
     buf_b[24:104, :] = jnp.where(inside_field(16, 80), pull, 0.0)
 
-    def weigh(i, carry):
-        start = pl.multiple_of((i + FIRST_BAND) * BAND, BAND)
-        value = 2.0 * field[:, pl.ds(start, BAND), :] * buf_b[pl.ds(start + 8, BAND), :][None] / KERNELS
-        rows = pl.ds(pl.multiple_of(i * CHANNELS * BAND, CHANNELS * BAND), CHANNELS * BAND)
-        products[rows, :] = value.reshape(CHANNELS * BAND, LANES).astype(BF16)
-        return carry
-
-    lax.fori_loop(0, LAST_BAND - FIRST_BAND + 1, weigh, 0)
-
-    def mix(g, carry):
-        rows = pl.ds(pl.multiple_of(g * CHANNELS * BAND, CHANNELS * BAND), 6 * CHANNELS * BAND)
-        value = jnp.dot(mixer[...], products[rows, :], preferred_element_type=F32)
+    def weigh(i):
+        start = (i + FIRST_BAND) * BAND
+        value = 2.0 * field[:, start : start + BAND, :] * buf_b[start + 8 : start + 8 + BAND, :][None] / KERNELS
+        rows = CHANNELS * BAND
+        products[i * rows : (i + 1) * rows, :] = value.reshape(rows, LANES).astype(BF16)
+
+    def mix(g):
+        rows = CHANNELS * BAND
+        value = jnp.dot(mixer[...], products[g * rows : (g + 6) * rows, :], preferred_element_type=F32)
         for i in range(2):
-            mixed[i, pl.ds(pl.multiple_of(g * 8 * PITCH, 8 * PITCH), 8 * PITCH), :] = value[:, i * 128 : (i + 1) * 128]
-        return carry
-
-    lax.fori_loop(0, ROWS // 8, mix, 0)
-
-    gradient = jnp.zeros((ROWS, 128), F32)
-    for t in range(TAPS):
-        part = jnp.concatenate([mixed[i, pl.ds(t, ROWS, stride=PITCH), :] for i in range(2)], axis=1)
-        gradient = gradient + pltpu.roll(part, 236 - t, 1)[:, 0:128]
-
-    def gather(sums, axis_size, me, number):
-        out = []
-        for d in range(1, axis_size):
-            peer = lax.rem(me + d, axis_size)
-            out.append(
-                pltpu.make_async_remote_copy(
-                    src_ref=sums.at[me],
-                    dst_ref=sums.at[me],
-                    send_sem=sum_send.at[number, d],
-                    recv_sem=sum_recv.at[number, d],
-                    device_id=(peer, gx) if number == 0 else (gy, peer),
-                    device_id_type=MESH,
-                )
-            )
-            out[-1].start()
-        for copy in out:
-            copy.wait()
-
+            mixed[i, g * 8 * PITCH : (g + 1) * 8 * PITCH, :] = value[:, i * 128 : (i + 1) * 128]
+
+    def gather_taps(g):
+        total = jnp.zeros((8, LANES), F32)
+        for t in range(TAPS):
+            rows = pl.ds(g * 8 * PITCH + t, 8, stride=PITCH)
+            part = jnp.concatenate([mixed[i, rows, :] for i in range(2)], axis=1)
+            total = total + pltpu.roll(part, 236 - t, 1)
+        return total[:, 0:128]
+
+    for i in range(5):
+        weigh(i)
+    parts = []
+    for g in range(ROWS // 8):
+        weigh(g + 5)
+        mix(g)
+        if g:
+            parts.append(gather_taps(g - 1))
+    parts.append(gather_taps(ROWS // 8 - 1))
+    gradient = jnp.concatenate(parts, axis=0)
+
+    inner = max(d for d in (1, 2, 4) if nx % d == 0)
+    outer = nx // inner
+
+    def ring(d, n):
+        return min(d, n - d)
+
+    def gather(sums, number):
+        if number == 0:
+            hops = [(ring(d, ny), d, 0) for d in range(1, ny)]
+        else:
+            hops = [(ring(a, outer) + ring(b, inner), a, b) for a in range(outer) for b in range(inner) if a or b]
+        me = gx if number else gy
+        for _, a, b in sorted(hops, reverse=True):
+            if number == 0:
+                device = at(a, 0)
+            else:
+                y, x = lax.rem(gx // inner + a, outer), lax.rem(lax.rem(gx, inner) + b, inner)
+                device = (gy, y * inner + x)
+            pltpu.make_async_remote_copy(
+                src_ref=sums.at[me],
+                dst_ref=sums.at[me],
+                send_sem=sum_send.at[number],
+                recv_sem=sum_recv.at[number],
+                device_id=device,
+                device_id_type=MESH,
+            ).start()
+        wait_all(sums.at[pl.ds(0, len(hops))], sum_send.at[number], sum_recv.at[number])
+
+    gradient_ref[...] = gradient
+    out = pltpu.make_async_copy(gradient_ref, gradient_hbm, input_sem.at[5])
+    out.start()
     square = jnp.sum(gradient * gradient, axis=0, keepdims=True)
     sums_y[gy, 0:1, :] = loss[:, 0:128] + loss[:, 128:256]
     sums_y[gy, 1:2, :] = square
-    gather(sums_y, ny, gy, 0)
+    gather(sums_y, 0)
+    learn(3)
     sums_x[gx] = jnp.sum(sums_y[...], axis=0)
-    gather(sums_x, nx, gx, 1)
-    totals = jnp.sum(jnp.sum(sums_x[...], axis=0), axis=1, keepdims=True)
+    gather(sums_x, 1)
+    sums_ref[...] = jnp.sum(sums_x[...], axis=0)
+    out.wait()
+
+
+def finish(pixels, mask_ref, gradient_ref, sums_ref, update_ref, loss_ref):
+    totals = jnp.sum(sums_ref[...], axis=1, keepdims=True)
     loss_ref[...] = totals[0:1, :]
-    scale = jnp.sqrt(totals[1:2, :] / (total_rows * total_cols) + 1e-06)
-    update_ref[...] = mask_ref[...] - gradient / scale
+    scale = jnp.sqrt(totals[1:2, :] / pixels + 1e-06)
+    update_ref[...] = mask_ref[...] - gradient_ref[...] / scale
 
 
 def solution(mesh):
@@ -380,21 +431,22 @@
     rows = CHANNELS * BAND
 
     def step(mask, target, kernels, offsets, load_weights):
-        update, loss = pl.pallas_call(
+        gradient, sums = pl.pallas_call(
             functools.partial(kernel, (ny, nx)),
             out_shape=(
                 jax.ShapeDtypeStruct((ROWS, COLS), F32),
-                jax.ShapeDtypeStruct((1, 1), F32),
+                jax.ShapeDtypeStruct((2, 128), F32),
             ),
             in_specs=[pl.BlockSpec(memory_space=pl.ANY)] * 5,
-            out_specs=(vmem, vmem),
+            out_specs=(pl.BlockSpec(memory_space=pl.ANY), vmem),
             scratch_shapes=[
                 pltpu.SMEM((2, LOAD_TAPS), jnp.int32),
                 pltpu.SMEM((LOAD_TAPS,), F32),
                 pltpu.VMEM((ROWS, COLS), F32),
                 pltpu.VMEM((ROWS, COLS), jnp.int32),
                 pltpu.VMEM((TAPS, CHANNELS, TAPS), BF16),
-                pltpu.SemaphoreType.DMA((5,)),
+                pltpu.VMEM((ROWS, COLS), F32),
+                pltpu.SemaphoreType.DMA((6,)),
                 pltpu.VMEM((2, ROWS, COLS), BF16),
                 pltpu.VMEM((2, ROWS, COLS), BF16),
                 pltpu.VMEM((3, 2, 16, COLS), BF16),
@@ -418,13 +470,23 @@
                 pltpu.VMEM((2, 136, 128), F32),
                 pltpu.VMEM((10 * rows, LANES), BF16),
                 pltpu.VMEM((2, ROWS * PITCH, 128), F32),
-                pltpu.SemaphoreType.DMA((14,)),
-                pltpu.SemaphoreType.DMA((14,)),
-                pltpu.SemaphoreType.DMA((2, 32)),
-                pltpu.SemaphoreType.DMA((2, 32)),
+                pltpu.SemaphoreType.DMA((3,)),
+                pltpu.SemaphoreType.DMA((3,)),
+                pltpu.SemaphoreType.DMA((2,)),
+                pltpu.SemaphoreType.DMA((2,)),
+                pltpu.SemaphoreType.REGULAR((2, 4)),
             ],
             compiler_params=pltpu.CompilerParams(collective_id=0, has_side_effects=True),
         )(offsets.T, load_weights, mask, target, kernels.transpose(1, 0, 2))
+        update, loss = pl.pallas_call(
+            functools.partial(finish, ny * ROWS * nx * COLS),
+            out_shape=(
+                jax.ShapeDtypeStruct((ROWS, COLS), F32),
+                jax.ShapeDtypeStruct((1, 1), F32),
+            ),
+            in_specs=[vmem] * 3,
+            out_specs=(vmem, vmem),
+        )(mask, gradient, sums)
         return update, loss[0, 0]
 
     placed = (P("gy", "gx"), P("gy", "gx"), P(), P(), P())

time: 43 us -> 38.4 us (0.89)
  between operations: 2.4 us -> 0.64 us
  Pallas kernels: 39 us -> 37.6 us
  local copies, waits for them, and re-layouts: 1.34 us -> 0 us
    pallas_call x1, Pallas kernels: 39 us -> 36.1 us  [step(): pl.pallas_call(functools.partial(kernel, (ny, nx)), out_shape=(jax.ShapeD...]
    pallas_call x0 -> x1, Pallas kernels: none -> 1.45 us  [step(): pl.pallas_call(functools.partial(finish, ny * ROWS * nx * COLS), out_shap...]
    unnamed x1 -> x0, local copies, waits for them, and re-layouts: 1.34 us -> none
where the time goes in v3:
time: 38.4 us; the launch traced here: 38.2 us
  Pallas kernels  37.6 us (98%)
  between operations  0.64 us (2%)
    pallas_call x1, Pallas kernels, step(): pl.pallas_call(functools.partial(kernel, (ny, nx)), out_shape=(jax.ShapeD...  36.1 us
    pallas_call x1, Pallas kernels, step(): pl.pallas_call(functools.partial(finish, ny * ROWS * nx * COLS), out_shap...  1.45 us

profile of v3, /device:TPU:1, one launch (start us, length us, event | category | flops | bytes accessed | tf_op | source)
XLA Modules:
  0.0 38.2 jit_solution(16224010216327451667)
XLA Ops:
  0.6 36.1 %shard_map.68 = (f32[40,128]{1,0:T(8,128)}, f32[2,128]{1,0:T(2,128)}) custom-call(s32[2,8]{1,0:T(2,128)} %bitcast.4, f32[8]{0:T(128)} %weights_hbm.1, f32[40,128]{1,0:T(8,128)} %mask_ref.1, s32[40,128]{1,0:T(8,128)} %target_hbm.1, bf16[35,24,35]{2,1,0:T(8,128)(2,1)} %bitcast.3), custom_call_target="tpu_custom_call" | custom-call | tf_op jit(solution)/shard_map/pallas_call | solution.py:434
  36.8 1.5 %shard_map.69 = (f32[40,128]{1,0:T(8,128)}, f32[1,1]{1,0:T(1,128)}) custom-call(f32[40,128]{1,0:T(8,128)} %mask_ref.1, f32[40,128]{1,0:T(8,128)} %get-tuple-element.6.gradient_ref, f32[2,128]{1,0:T(2,128)} %get-tuple-element.7.sums_ref), custom_call_target="tpu_custom_call" | custom-call | tf_op jit(solution)/shard_map/pallas_call | solution.py:481

commit v4 on v3

--- a/solution.py
+++ b/solution.py
@@ -40,16 +40,21 @@
     return lax.broadcasted_iota(jnp.int32, (rows, lanes), 0)
 
 
-def smooth(ref, start, rows):
-    down = sum(SMOOTH_TAPS[a] * ref[pl.ds(start + a - 2, rows), :] for a in range(5))
+def rows_from(halves, start, rows):
+    return jnp.concatenate([halves[i, pl.ds(start, rows), :] for i in range(2)], axis=1)
+
+
+def rows_to(halves, start, value):
+    for i in range(2):
+        halves[i, start : start + value.shape[0], :] = value[:, i * 128 : (i + 1) * 128]
+
+
+def smooth(halves, start, rows):
+    down = sum(SMOOTH_TAPS[a] * rows_from(halves, start + a - 2, rows) for a in range(5))
     total = SMOOTH_TAPS[2] * down
     for b in (0, 1, 3, 4):
         total = total + SMOOTH_TAPS[b] * pltpu.roll(down, (2 - b) % LANES, 1)
     return total
-
-
-def rows_from(halves, start, rows):
-    return jnp.concatenate([halves[i, pl.ds(start, rows), :] for i in range(2)], axis=1)
 
 
 def build_taps(kernels_ref, taps32, taps):
@@ -96,14 +101,13 @@
     mask_hbm,
     target_hbm,
     kernels_hbm,
-    gradient_hbm,
+    mask_ref,
+    gradient_ref,
     sums_ref,
     offsets_ref,
     weights_ref,
-    mask_ref,
     target_ref,
     kernels_ref,
-    gradient_ref,
     input_sem,
     whole,
     edges,
@@ -121,11 +125,10 @@
     wanted,
     patches,
     field,
-    buf_a,
-    buf_b,
-    buf_c,
-    halves_b,
-    halves_c,
+    dim,
+    lit,
+    rest,
+    pull,
     products,
     mixed,
     send_sem,
@@ -230,9 +233,7 @@
     tell(2)
     inputs[3].wait()
     inputs[4].wait()
-    for ref in (buf_a, buf_b, buf_c):
-        ref[0:8, :] = jnp.zeros((8, LANES), F32)
-        ref[8 + BANDS * BAND :, :] = jnp.zeros((8, LANES), F32)
+    rows_to(pull, 16, jnp.zeros((8, LANES), F32))
     patches[152 * PITCH :, :] = jnp.zeros((96, LANES), BF16)
     for kind, ref in enumerate((got_edges, got_rims, got_whole)):
         wait_all(ref, send_sem.at[kind], recv_sem.at[kind])
@@ -265,8 +266,8 @@
     def framed_target(row, middle, west, east):
         n = lane_index(ROWS, 128)
         moved = pltpu.roll(middle, FIELD_MARGIN, 1)
-        wanted[row : row + ROWS, 0:128] = jnp.where(n < FIELD_MARGIN, pltpu.roll(west, 74, 1), moved)
-        wanted[row : row + ROWS, 128:256] = jnp.where(n < FIELD_MARGIN, moved, pltpu.roll(east, 101, 1))
+        wanted[0, row : row + ROWS, :] = jnp.where(n < FIELD_MARGIN, pltpu.roll(west, 74, 1), moved)
+        wanted[1, row : row + ROWS, :] = jnp.where(n < FIELD_MARGIN, moved, pltpu.roll(east, 101, 1))
 
     framed_target(0, wide(got_whole[0, 1]), wide(got_edges[0, 0]), wide(got_edges[1, 0]))
     framed_target(40, own_target, wide(got_edges[0, 1]), wide(got_edges[1, 1]))
@@ -301,7 +302,7 @@
         if FIRST_BAND <= i <= LAST_BAND:
             field[:, start : start + BAND, :] = value
         intensity = jnp.sum(value * value, axis=0) / KERNELS
-        buf_a[start + 8 : start + 8 + BAND, :] = jnp.where(inside_field(start, BAND), intensity, 0.0)
+        rows_to(dim, start + 6, jnp.where(inside_field(start, BAND), intensity, 0.0))
 
     for i in range(BANDS):
         if i + 6 < 19:
@@ -311,43 +312,34 @@
             learn(2)
             tell(3)
 
-    dense = smooth(buf_a, 8, 120)
-    develop = jnp.where(inside_field(0, 120), jax.nn.sigmoid(SHARPNESS * (dense - THRESHOLD)), 0.0)
-    buf_b[8:128, :] = develop
-    for i in range(2):
-        halves_b[i, 8:128, :] = develop[:, i * 128 : (i + 1) * 128]
-        halves_b[i, 0:8, :] = jnp.zeros((8, 128), F32)
-        halves_b[i, 128:136, :] = jnp.zeros((8, 128), F32)
-
-    loading = jnp.zeros((104, LANES), F32)
+    dense = smooth(dim, 8, 112)
+    rows_to(lit, 8, jnp.where(inside_field(2, 112), jax.nn.sigmoid(SHARPNESS * (dense - THRESHOLD)), 0.0))
+
+    loading = jnp.zeros((96, LANES), F32)
     for j in range(LOAD_TAPS):
-        part = rows_from(halves_b, 16 + offsets_ref[0, j], 104)
+        part = rows_from(lit, 16 + offsets_ref[0, j], 96)
         loading = loading + weights_ref[j] * pltpu.roll(part, lax.rem(LANES - offsets_ref[1, j], LANES), 1)
-    printed = buf_b[16:120, :] - LOADING_GAIN / LOAD_TAPS * loading
-    y = first_row - FIELD_MARGIN + 8 + row_index(104)
-    x = first_col - FIELD_MARGIN + lane_index(104)
+    printed = rows_from(lit, 16, 96) - LOADING_GAIN / LOAD_TAPS * loading
+    y = first_row - FIELD_MARGIN + 10 + row_index(96)
+    x = first_col - FIELD_MARGIN + lane_index(96)
     weight = (1.0 + 2.0 * y.astype(F32) / total_rows) * (1.0 + 2.0 * x.astype(F32) / total_cols)
-    diff = printed - wanted[11:115, :]
+    diff = printed - rows_from(wanted, 13, 96)
     own = (y >= first_row) & (y < first_row + ROWS) & (x >= first_col) & (x < first_col + COLS)
     loss = jnp.sum(jnp.where(own, weight * diff * diff, 0.0), axis=0, keepdims=True)
-    resid = jnp.where(inside_field(8, 104), 2.0 * weight * diff, 0.0)
-    buf_c[16:120, :] = resid
-    for i in range(2):
-        halves_c[i, 16:120, :] = resid[:, i * 128 : (i + 1) * 128]
-
-    back = jnp.zeros((88, LANES), F32)
+    rows_to(rest, 16, jnp.where(inside_field(10, 96), 2.0 * weight * diff, 0.0))
+
+    back = jnp.zeros((80, LANES), F32)
     for j in range(LOAD_TAPS):
-        part = rows_from(halves_c, 24 - offsets_ref[0, j], 88)
+        part = rows_from(rest, 24 - offsets_ref[0, j], 80)
         back = back + weights_ref[j] * pltpu.roll(part, lax.rem(LANES + offsets_ref[1, j], LANES), 1)
-    slope = buf_c[24:112, :] - LOADING_GAIN / LOAD_TAPS * back
-    nearby = buf_b[24:112, :]
-    buf_a[24:112, :] = slope * SHARPNESS * nearby * (1.0 - nearby)
-    pull = smooth(buf_a, 24, 80)
-    buf_b[24:104, :] = jnp.where(inside_field(16, 80), pull, 0.0)
+    slope = rows_from(rest, 24, 80) - LOADING_GAIN / LOAD_TAPS * back
+    nearby = rows_from(lit, 24, 80)
+    rows_to(dim, 24, slope * SHARPNESS * nearby * (1.0 - nearby))
+    rows_to(pull, 24, jnp.where(inside_field(18, 80), (2.0 / KERNELS) * smooth(dim, 24, 80), 0.0))
 
     def weigh(i):
         start = (i + FIRST_BAND) * BAND
-        value = 2.0 * field[:, start : start + BAND, :] * buf_b[start + 8 : start + 8 + BAND, :][None] / KERNELS
+        value = field[:, start : start + BAND, :] * rows_from(pull, start + 6, BAND)[None]
         rows = CHANNELS * BAND
         products[i * rows : (i + 1) * rows, :] = value.reshape(rows, LANES).astype(BF16)
 
@@ -405,8 +397,6 @@
         wait_all(sums.at[pl.ds(0, len(hops))], sum_send.at[number], sum_recv.at[number])
 
     gradient_ref[...] = gradient
-    out = pltpu.make_async_copy(gradient_ref, gradient_hbm, input_sem.at[5])
-    out.start()
     square = jnp.sum(gradient * gradient, axis=0, keepdims=True)
     sums_y[gy, 0:1, :] = loss[:, 0:128] + loss[:, 128:256]
     sums_y[gy, 1:2, :] = square
@@ -415,7 +405,6 @@
     sums_x[gx] = jnp.sum(sums_y[...], axis=0)
     gather(sums_x, 1)
     sums_ref[...] = jnp.sum(sums_x[...], axis=0)
-    out.wait()
 
 
 def finish(pixels, mask_ref, gradient_ref, sums_ref, update_ref, loss_ref):
@@ -431,22 +420,21 @@
     rows = CHANNELS * BAND
 
     def step(mask, target, kernels, offsets, load_weights):
-        gradient, sums = pl.pallas_call(
+        held, gradient, sums = pl.pallas_call(
             functools.partial(kernel, (ny, nx)),
             out_shape=(
-                jax.ShapeDtypeStruct((ROWS, COLS), F32),
-                jax.ShapeDtypeStruct((2, 128), F32),
+                pltpu.VMEM((ROWS, COLS), F32),
+                pltpu.VMEM((ROWS, COLS), F32),
+                pltpu.VMEM((2, 128), F32),
             ),
             in_specs=[pl.BlockSpec(memory_space=pl.ANY)] * 5,
-            out_specs=(pl.BlockSpec(memory_space=pl.ANY), vmem),
+            out_specs=(vmem, vmem, vmem),
             scratch_shapes=[
                 pltpu.SMEM((2, LOAD_TAPS), jnp.int32),
                 pltpu.SMEM((LOAD_TAPS,), F32),
-                pltpu.VMEM((ROWS, COLS), F32),
                 pltpu.VMEM((ROWS, COLS), jnp.int32),
                 pltpu.VMEM((TAPS, CHANNELS, TAPS), BF16),
-                pltpu.VMEM((ROWS, COLS), F32),
-                pltpu.SemaphoreType.DMA((6,)),
+                pltpu.SemaphoreType.DMA((5,)),
                 pltpu.VMEM((2, ROWS, COLS), BF16),
                 pltpu.VMEM((2, ROWS, COLS), BF16),
                 pltpu.VMEM((3, 2, 16, COLS), BF16),
@@ -460,14 +448,13 @@
                 pltpu.VMEM((6 * rows, 384), F32),
                 pltpu.VMEM((8 * PITCH, 6 * rows), BF16),
                 pltpu.VMEM((160, LANES), F32),
-                pltpu.VMEM((120, LANES), F32),
+                pltpu.VMEM((2, 120, 128), F32),
                 pltpu.VMEM((152 * PITCH + 96, LANES), BF16),
                 pltpu.VMEM((CHANNELS, BANDS * BAND, LANES), F32),
-                pltpu.VMEM((136, LANES), F32),
-                pltpu.VMEM((136, LANES), F32),
-                pltpu.VMEM((136, LANES), F32),
-                pltpu.VMEM((2, 136, 128), F32),
-                pltpu.VMEM((2, 136, 128), F32),
+                pltpu.VMEM((2, 128, 128), F32),
+                pltpu.VMEM((2, 128, 128), F32),
+                pltpu.VMEM((2, 128, 128), F32),
+                pltpu.VMEM((2, 128, 128), F32),
                 pltpu.VMEM((10 * rows, LANES), BF16),
                 pltpu.VMEM((2, ROWS * PITCH, 128), F32),
                 pltpu.SemaphoreType.DMA((3,)),
@@ -486,7 +473,7 @@
             ),
             in_specs=[vmem] * 3,
             out_specs=(vmem, vmem),
-        )(mask, gradient, sums)
+        )(*(pltpu.with_memory_space_constraint(a, pltpu.VMEM) for a in (held, gradient, sums)))
         return update, loss[0, 0]
 
     placed = (P("gy", "gx"), P("gy", "gx"), P(), P(), P())

time: 38.4 us -> 36.9 us (0.961)
  Pallas kernels: 37.6 us -> 36.2 us
    pallas_call x1, Pallas kernels: 1.45 us -> 0.71 us  [step(): pl.pallas_call(functools.partial(finish, ny * ROWS * nx * COLS), out_shap...]
    pallas_call x1, Pallas kernels: 36.1 us -> 35.5 us  [step(): pl.pallas_call(functools.partial(kernel, (ny, nx)), out_shape=(pltpu.VMEM...]
where the time goes in v4:
time: 36.9 us; the launch traced here: 36.8 us
  Pallas kernels  36.2 us (98%)
  between operations  0.64 us (2%)
    pallas_call x1, Pallas kernels, step(): pl.pallas_call(functools.partial(kernel, (ny, nx)), out_shape=(pltpu.VMEM...  35.5 us

profile of v4, /device:TPU:1, one launch (start us, length us, event | category | flops | bytes accessed | tf_op | source)
XLA Modules:
  0.0 36.8 jit_solution(10600316042912304522)
XLA Ops:
  0.6 35.5 %shard_map.68 = (f32[40,128]{1,0:T(8,128)S(1)}, f32[40,128]{1,0:T(8,128)S(1)}, f32[2,128]{1,0:T(2,128)S(1)}) custom-call(s32[2,8]{1,0:T(2,128)} %bitcast.4, f32[8]{0:T(128)} %weights_hbm.1, f32[40,128]{1,0:T(8,128)} %mask_hbm.1, s32[40,128]{1,0:T(8,128)} %target_hbm.1, bf16[35,24,35]{2,1,0:T(8,128)(2,1)} %bitcast.3), custom_call_target="tpu_custom_call" | custom-call | tf_op jit(solution)/shard_map/pallas_call | solution.py:423
  36.1 0.7 %shard_map.69 = (f32[40,128]{1,0:T(8,128)}, f32[1,1]{1,0:T(1,128)}) custom-call(f32[40,128]{1,0:T(8,128)S(1)} %get-tuple-element.7.mask_ref, f32[40,128]{1,0:T(8,128)S(1)} %get-tuple-element.8.gradient_ref, f32[2,128]{1,0:T(2,128)S(1)} %get-tuple-element.9.sums_ref), custom_call_target="tpu_custom_call" | custom-call | tf_op jit(solution)/shard_map/pallas_call | solution.py:468

commit v5 on v4

--- a/solution.py
+++ b/solution.py
@@ -162,8 +162,8 @@
     for dy, dx in peers:
         pl.semaphore_signal(barrier, inc=1, device_id=at(dy, dx), device_id_type=MESH)
 
-    rounds_y = [r for r in (2, 4, 8) if 2 * r < ny]
-    rounds_x = [r for r in (1, 2, 4, 8) if 2 * r < nx]
+    rounds_y = [r for r in (4, 8) if 2 * r < ny]
+    rounds_x = [r for r in (2, 4, 8) if 2 * r < nx]
 
     def tell(number):
         for along_x, rounds in ((0, rounds_y), (1, rounds_x)):
@@ -209,34 +209,35 @@
             device_id_type=MESH,
         ).start()
 
+    def send_rim(dy, dx):
+        end = 0 if dy == 2 else 1
+        send(1, rims.at[1 - dx, end], got_rims.at[1 - dx, end], dy, dx)
+
     def wait_all(ref, sent, received):
         for sem in (sent, received):
             pltpu.make_async_copy(ref, ref, sem).wait()
 
     for dx in (1, -1):
-        side = 1 if dx == 1 else 0
-        for dy in (-1, 0, 1):
-            send(0, edges.at[side], got_edges.at[0 if dx == 1 else 1, 1 - dy], dy, dx)
-    for dx in (1, -1, 0):
         for dy in (2, -2):
-            end = 0 if dy == 2 else 1
-            send(1, rims.at[1 - dx, end], got_rims.at[1 - dx, end], dy, dx)
+            send_rim(dy, dx)
+    for dy in (-1, 1, 0):
+        for dx in (1, -1):
+            side = 0 if dx == 1 else 1
+            send(0, edges.at[1 - side], got_edges.at[side, 1 - dy], dy, dx)
     for dy in (1, -1):
         send(2, whole, got_whole.at[0 if dy == 1 else 1], dy, 0)
-    tell(0)
+    for dy in (2, -2):
+        send_rim(dy, 0)
     inputs[2].wait()
     build_taps(kernels_ref, taps32, taps)
-    learn(0)
-    tell(1)
     build_mixer(taps32, mixer32, mixer)
-    learn(1)
-    tell(2)
     inputs[3].wait()
     inputs[4].wait()
     rows_to(pull, 16, jnp.zeros((8, LANES), F32))
     patches[152 * PITCH :, :] = jnp.zeros((96, LANES), BF16)
     for kind, ref in enumerate((got_edges, got_rims, got_whole)):
         wait_all(ref, send_sem.at[kind], recv_sem.at[kind])
+    tell(0)
 
     first_row = gy * ROWS
     first_col = gx * COLS
@@ -308,9 +309,8 @@
         if i + 6 < 19:
             spread(i + 6)
         band(i)
-        if i == 9:
-            learn(2)
-            tell(3)
+    learn(0)
+    tell(1)
 
     dense = smooth(dim, 8, 112)
     rows_to(lit, 8, jnp.where(inside_field(2, 112), jax.nn.sigmoid(SHARPNESS * (dense - THRESHOLD)), 0.0))
@@ -400,8 +400,10 @@
     square = jnp.sum(gradient * gradient, axis=0, keepdims=True)
     sums_y[gy, 0:1, :] = loss[:, 0:128] + loss[:, 128:256]
     sums_y[gy, 1:2, :] = square
+    learn(1)
+    tell(2)
     gather(sums_y, 0)
-    learn(3)
+    learn(2)
     sums_x[gx] = jnp.sum(sums_y[...], axis=0)
     gather(sums_x, 1)
     sums_ref[...] = jnp.sum(sums_x[...], axis=0)
@@ -461,7 +463,7 @@
                 pltpu.SemaphoreType.DMA((3,)),
                 pltpu.SemaphoreType.DMA((2,)),
                 pltpu.SemaphoreType.DMA((2,)),
-                pltpu.SemaphoreType.REGULAR((2, 4)),
+                pltpu.SemaphoreType.REGULAR((2, 3)),
             ],
             compiler_params=pltpu.CompilerParams(collective_id=0, has_side_effects=True),
         )(offsets.T, load_weights, mask, target, kernels.transpose(1, 0, 2))

time: 36.9 us -> 36.3 us (0.984)
  Pallas kernels: 36.2 us -> 35.6 us
    pallas_call x1, Pallas kernels: 35.5 us -> 34.8 us  [step(): pl.pallas_call(functools.partial(kernel, (ny, nx)), out_shape=(pltpu.VMEM...]
where the time goes in v5:
time: 36.3 us; the launch traced here: 36.2 us
  Pallas kernels  35.6 us (98%)
  between operations  0.64 us (2%)
    pallas_call x1, Pallas kernels, step(): pl.pallas_call(functools.partial(kernel, (ny, nx)), out_shape=(pltpu.VMEM...  34.8 us

profile of v5, /device:TPU:1, one launch (start us, length us, event | category | flops | bytes accessed | tf_op | source)
XLA Modules:
  0.0 36.2 jit_solution(849631751316595858)
XLA Ops:
  0.6 34.8 %shard_map.68 = (f32[40,128]{1,0:T(8,128)S(1)}, f32[40,128]{1,0:T(8,128)S(1)}, f32[2,128]{1,0:T(2,128)S(1)}) custom-call(s32[2,8]{1,0:T(2,128)} %bitcast.4, f32[8]{0:T(128)} %weights_hbm.1, f32[40,128]{1,0:T(8,128)} %mask_hbm.1, s32[40,128]{1,0:T(8,128)} %target_hbm.1, bf16[35,24,35]{2,1,0:T(8,128)(2,1)} %bitcast.3), custom_call_target="tpu_custom_call" | custom-call | tf_op jit(solution)/shard_map/pallas_call | solution.py:425
  35.5 0.7 %shard_map.69 = (f32[40,128]{1,0:T(8,128)}, f32[1,1]{1,0:T(1,128)}) custom-call(f32[40,128]{1,0:T(8,128)S(1)} %get-tuple-element.7.mask_ref, f32[40,128]{1,0:T(8,128)S(1)} %get-tuple-element.8.gradient_ref, f32[2,128]{1,0:T(2,128)S(1)} %get-tuple-element.9.sums_ref), custom_call_target="tpu_custom_call" | custom-call | tf_op jit(solution)/shard_map/pallas_call | solution.py:470
